TPU v7x, 256 devices: a whole 4x4x8 slice. The times are simulated.
256 devices in a mesh: dp: 32 (over z_hi, y, x), tensor: 8 (over z_lo, core).
Axes of the slice: x: 4, y: 4, z: 8 (z_hi: 2, z_lo: 4; z = z_hi * 4 + z_lo), core: 2. Of those that a mesh axis runs over, the one named last changes fastest.
Arguments:
- queries: bfloat16 [32768, 3072], P('dp', 'tensor'), may hold values from -70 to 70
- keys: bfloat16 [32768, 3072], P('dp', 'tensor'), may hold values from -5 to 5
- values: bfloat16 [32768, 3072], P('dp', 'tensor'), may hold values from -6 to 6
- out_gradient: bfloat16 [32768, 5120], P(('dp', 'tensor')), may hold values from -24 to 24
- out_weight: bfloat16 [3072, 5120], P('tensor'), may hold values from -0.109375 to 0.109375
- segments: int32 [32, 8], replicated, may hold values from 0 to 7, as said below
- counts: int32 [32], replicated, may hold values from 1 to 4, as said below
Outputs:
- query_gradient: bfloat16 [32768, 3072], P('dp', 'tensor')
- key_gradient: bfloat16 [32768, 3072], P('dp', 'tensor')
- value_gradient: bfloat16 [32768, 3072], P('dp', 'tensor')
- weight_gradient: float32 [5120, 3072], P('dp', 'tensor')
Inputs may be any that keep to these rules, and one draw needn't show every extreme that they name: `segments`: along each row ids never fall; each protein spans 1 to 4 consecutive blocks, and some protein spans exactly 4; the last counts[r] blocks of replica r are whole proteins. counts[r] equals counts[(r + 16) mod 32].
All inputs are finite; a program needn't handle non-finite values.
Results may differ from a plain program's by a relative error of at most 0.025.
Values may be sent and summed in bfloat16 or wider, within the bound.
No kernel may reach another device: no remote copies, remote signals or barrier semaphores. Data moves between devices by JAX's collectives and lax.ppermute only.
A program may use at most 128 MiB of HBM per device.

v0:
```python
import functools

import jax
import jax.numpy as jnp
from jax import lax
from jax.experimental import pallas as pl
from jax.experimental.pallas import tpu as pltpu
from jax.sharding import Mesh
from jax.sharding import PartitionSpec as P


HEAD_SIZE = 128
BLOCK = 128
WINDOW = 4
MOVABLE = 4
CHIPS = 4
REPLICAS = 32
SCALE = HEAD_SIZE**-0.5
LOG2E = 1.4426950408889634
DP = ("z_hi", "y", "x")
TENSOR = ("z_lo", "core")
AXES = DP + TENSOR

masked_score = -1e30


def swapped(x, axis):
    n = lax.axis_size(axis)
    return lax.ppermute(x, axis, [(i, (i + n // 2) % n) for i in range(n)])


def dot(a, b, over):
    return lax.dot_general(
        a, b, (((over[0],), (over[1],)), ((), ())), preferred_element_type=jnp.float32
    )


def cost(flops, moved, transcendentals=0):
    return pl.CostEstimate(flops=flops, bytes_accessed=moved, transcendentals=transcendentals)


def block_at(index, size=BLOCK):
    return pl.ds(pl.multiple_of(index * size, size), size)


def window_of(ids, row, b):
    blocks = ids.shape[1]
    own = ids[row, b]
    first = jnp.int32(0)
    for j in range(blocks):
        first = first + jnp.where(ids[row, j] < own, 1, 0)
    start = jnp.minimum(first, blocks - WINDOW)
    return own, start, pl.ds(pl.multiple_of(start * BLOCK, BLOCK), WINDOW * BLOCK)


def forward_kernel(here_ref, ids_ref, q_ref, k_ref, v_ref, p_ref, o_ref, r_ref):
    row, chip, core = here_ref[0], here_ref[1], here_ref[2]
    for b in range(ids_ref.shape[1]):
        own, start, near = window_of(ids_ref, row, b)
        rows = pl.ds(b * BLOCK, BLOCK)
        scores = dot(q_ref[rows, :], k_ref[near, :], (1, 1))
        tiles = []
        for t in range(WINDOW):
            off = jnp.where(ids_ref[row, start + t] == own, 0.0, masked_score)
            tiles.append(scores[:, t * BLOCK : (t + 1) * BLOCK] + off)
        top = jnp.max(functools.reduce(jnp.maximum, tiles), axis=1, keepdims=True)
        tiles = [jnp.exp2((x - top) * (SCALE * LOG2E)) for x in tiles]
        total = jnp.sum(functools.reduce(jnp.add, tiles), axis=1, keepdims=True)
        inverse = 1.0 / total
        p = jnp.concatenate([(x * inverse).astype(jnp.bfloat16) for x in tiles], axis=1)
        p_ref[0, rows, :] = p
        o = dot(p, v_ref[near, :], (1, 0)).astype(jnp.bfloat16)
        o_ref[rows, :] = o
        turn = lax.rem(chip + CHIPS - b // 2, CHIPS)
        r_ref[block_at(2 * turn + jnp.where(core == b % 2, 0, 1)), :] = o


def backward_kernel(
    here_ref, ids_ref, q_ref, k_ref, v_ref, g_ref, o_ref, p_ref,
    dq_ref, dk_ref, dv_ref, tail_ref, ka, va,
):
    row = here_ref[0]
    front = dq_ref.shape[0] - tail_ref.shape[1]
    ka[...] = jnp.zeros_like(ka)
    va[...] = jnp.zeros_like(va)
    for b in range(ids_ref.shape[1]):
        _, _, near = window_of(ids_ref, row, b)
        rows = pl.ds(b * BLOCK, BLOCK)
        g = g_ref[rows, :]
        p = p_ref[0, rows, :]
        dp = dot(g, v_ref[near, :], (1, 1))
        center = jnp.sum(
            g.astype(jnp.float32) * o_ref[rows, :].astype(jnp.float32), axis=1, keepdims=True
        )
        ds = (p.astype(jnp.float32) * (dp - center)).astype(jnp.bfloat16)
        dq_ref[rows, :] = (dot(ds, k_ref[near, :], (1, 0)) * SCALE).astype(jnp.bfloat16)
        ka[near, :] += dot(ds, q_ref[rows, :], (0, 0))
        va[near, :] += dot(p, g, (0, 0))
    dk_ref[...] = (ka[...] * SCALE).astype(jnp.bfloat16)
    dv_ref[...] = va[...].astype(jnp.bfloat16)
    for i, ref in enumerate((dq_ref, dk_ref, dv_ref)):
        tail_ref[i] = ref[front:, :]


def settle_kernel(here_ref, counts_ref, *refs):
    arrived_ref, outs, sems = refs[3], refs[4:7], refs[7]
    moving = counts_ref[here_ref[0]]
    front = outs[0].shape[0] - arrived_ref.shape[1]

    def copy(i, b):
        return pltpu.make_async_copy(
            arrived_ref.at[i, pl.ds(b * BLOCK, BLOCK), :],
            outs[i].at[pl.ds(front + b * BLOCK, BLOCK), :],
            sems.at[i, b],
        )

    for b in range(MOVABLE):

        @pl.when(b >= MOVABLE - moving)
        def _():
            for i in range(3):
                copy(i, b).start()

    for b in range(MOVABLE):

        @pl.when(b >= MOVABLE - moving)
        def _():
            for i in range(3):
                copy(i, b).wait()


def room(mebibytes):
    return pltpu.CompilerParams(vmem_limit_bytes=mebibytes * 2**20)


def prefetched(scalars, grid, in_specs, out_specs, scratch_shapes=()):
    return pltpu.PrefetchScalarGridSpec(
        num_scalar_prefetch=scalars,
        grid=grid,
        in_specs=in_specs,
        out_specs=out_specs,
        scratch_shapes=scratch_shapes,
    )


ANY = pl.BlockSpec(memory_space=pl.ANY)


def forward(here, ids, q, k, v):
    rows, inner = q.shape
    heads = inner // HEAD_SIZE
    keys = WINDOW * BLOCK
    hs = pl.BlockSpec((rows, HEAD_SIZE), lambda h, *_: (0, h))
    out = jax.ShapeDtypeStruct((rows, inner), jnp.bfloat16)
    return pl.pallas_call(
        forward_kernel,
        grid_spec=prefetched(
            2, (heads,), [hs] * 3, [pl.BlockSpec((1, rows, keys), lambda h, *_: (h, 0, 0)), hs, hs]
        ),
        out_shape=[jax.ShapeDtypeStruct((heads, rows, keys), jnp.bfloat16), out, out],
        cost_estimate=cost(
            4 * rows * keys * inner,
            10 * rows * inner + 2 * heads * rows * keys,
            heads * rows * keys,
        ),
        compiler_params=room(20),
        name="forward",
    )(here, ids, q, k, v)


def backward(here, ids, q, k, v, g, o, p):
    rows, inner = q.shape
    heads = inner // HEAD_SIZE
    keys = WINDOW * BLOCK
    moving = MOVABLE * BLOCK
    hs = pl.BlockSpec((rows, HEAD_SIZE), lambda h, *_: (0, h))
    return pl.pallas_call(
        backward_kernel,
        grid_spec=prefetched(
            2,
            (heads,),
            [hs] * 5 + [pl.BlockSpec((1, rows, keys), lambda h, *_: (h, 0, 0))],
            [hs] * 3 + [pl.BlockSpec((3, moving, HEAD_SIZE), lambda h, *_: (0, 0, h))],
            [pltpu.VMEM((rows, HEAD_SIZE), jnp.float32)] * 2,
        ),
        out_shape=[jax.ShapeDtypeStruct((rows, inner), jnp.bfloat16)] * 3
        + [jax.ShapeDtypeStruct((3, moving, inner), jnp.bfloat16)],
        compiler_params=room(20),
        cost_estimate=cost(8 * rows * keys * inner, 19 * rows * inner + 2 * heads * rows * keys),
        name="backward",
    )(here, ids, q, k, v, g, o, p)


def settle(here, counts, local, arrived):
    return pl.pallas_call(
        settle_kernel,
        grid_spec=prefetched(
            2,
            (1,),
            [ANY] * 3 + [pl.BlockSpec(memory_space=pltpu.VMEM)],
            [ANY] * 3,
            [pltpu.SemaphoreType.DMA((3, MOVABLE))],
        ),
        out_shape=[jax.ShapeDtypeStruct(x.shape, x.dtype) for x in local],
        input_output_aliases={2 + i: i for i in range(3)},
        compiler_params=room(8),
        cost_estimate=cost(0, 4 * arrived.size),
        name="settle",
    )(here, counts, *local, arrived)


def project_kernel(last, here_ref, *refs):
    pieces, w_ref = refs[: 2 * CHIPS], refs[2 * CHIPS]
    out_ref, acc = refs[-2:]
    step = pl.program_id(0)
    part = dot(jnp.concatenate([ref[...] for ref in pieces], axis=0), w_ref[...], (1, 1))
    chained = len(refs) == 2 * CHIPS + 4

    @pl.when(step == 0)
    def _():
        acc[...] = refs[2 * CHIPS + 1][...] + part if chained else part

    @pl.when(step > 0)
    def _():
        acc[...] += part

    @pl.when(step == pl.num_programs(0) - 1)
    def _():
        if not last:
            out_ref[...] = acc[...]
            return
        chip, core = here_ref[1], here_ref[2]
        for i in range(2 * CHIPS):
            source = lax.rem(chip + CHIPS - i // 2, CHIPS)
            block = 2 * source + (core if i % 2 == 0 else 1 - core)
            out_ref[block_at(block), :] = acc[i * BLOCK : (i + 1) * BLOCK].astype(jnp.bfloat16)


def piece_specs(pieces, first, width):
    def spec(i):
        at = first // width if i < 2 else 0
        return pl.BlockSpec((pieces[i].shape[0], width), lambda j, *_: (0, at + j))

    return [spec(i) for i in range(len(pieces))]


def project(here, pieces, first, width, w, before, last):
    depth = pieces[2].shape[1]
    rows = sum(x.shape[0] for x in pieces)
    inner = w.shape[0]
    at = first // width
    whole = pl.BlockSpec((rows, inner), lambda j, *_: (0, 0))
    in_specs = piece_specs(pieces, first, width)
    in_specs.append(pl.BlockSpec((inner, width), lambda j, *_: (0, at + j)))
    operands = [*pieces, w]
    if before is not None:
        in_specs.append(whole)
        operands.append(before)
    return pl.pallas_call(
        functools.partial(project_kernel, last),
        grid_spec=prefetched(
            1, (depth // width,), in_specs, whole, [pltpu.VMEM((rows, inner), jnp.float32)]
        ),
        out_shape=jax.ShapeDtypeStruct((rows, inner), jnp.bfloat16 if last else jnp.float32),
        cost_estimate=cost(
            2 * rows * depth * inner, 2 * rows * depth + 2 * inner * depth + 8 * rows * inner
        ),
        compiler_params=room(30),
        name="project",
    )(here, *operands)


def weight_kernel(here_ref, *refs):
    pieces, h_ref, out_ref = refs[: 2 * CHIPS], refs[2 * CHIPS], refs[-1]
    g = jnp.concatenate([ref[...] for ref in pieces], axis=0)
    out_ref[...] = (dot(g, h_ref[...], (0, 0)) * (1.0 / REPLICAS)).astype(jnp.bfloat16)


def weight(here, pieces, first, width, h):
    depth = pieces[2].shape[1]
    rows, inner = h.shape
    in_specs = piece_specs(pieces, first, width)
    in_specs.append(pl.BlockSpec((rows, inner), lambda j, *_: (0, 0)))
    return pl.pallas_call(
        weight_kernel,
        grid_spec=prefetched(
            1,
            (depth // width,),
            in_specs,
            pl.BlockSpec((width, inner), lambda j, *_: (j, 0)),
        ),
        out_shape=jax.ShapeDtypeStruct((depth, inner), jnp.bfloat16),
        compiler_params=room(26),
        cost_estimate=cost(
            2 * rows * depth * inner, 2 * rows * depth + 2 * depth * inner + 2 * rows * inner
        ),
        name="weight",
    )(here, *pieces, h)


def after(x, *others):
    return lax.optimization_barrier((x, *others))[0]


def steps(queries, keys, values, out_gradient, out_weight, segments, counts):
    depth = out_gradient.shape[1]
    half = depth // 2
    here = jnp.stack([lax.axis_index(DP), lax.axis_index("z_lo"), lax.axis_index("core")])
    here = here.astype(jnp.int32)
    ring = [(i, (i + 1) % CHIPS) for i in range(CHIPS)]

    own = [lax.slice_in_dim(out_gradient, c * half, (c + 1) * half, axis=1) for c in range(2)]
    partner = swapped(out_gradient, "core")
    pieces = [[out_gradient, partner] for _ in range(2)]

    def turn(c, x):
        y = lax.ppermute(x, "z_lo", ring)
        z = swapped(y, "core")
        pieces[c] += [y, z]
        return y

    first = turn(0, own[0])
    second = turn(0, first)
    turn(0, second)
    x = after(own[1], second)
    for _ in range(3):
        x = turn(1, x)

    chances, head_output, output_turned = forward(here, segments, queries, keys, values)

    gradient = None
    for c in range(2):
        gradient = project(here, pieces[c], c * half, 1280, out_weight, gradient, c == 1)

    sums = []
    for c in range(2):
        term = weight(here, pieces[c], c * half, 1280, output_turned)
        tiles = term.reshape(16, -1, term.shape[1])
        tiles = lax.all_to_all(tiles, ("y", "x"), 0, 0, tiled=True)
        sums.append(jnp.sum(tiles.astype(jnp.float32), axis=0))
    upper = lax.axis_index("z_hi") == 1
    kept = jnp.where(upper, sums[1], sums[0])
    sent = jnp.where(upper, sums[0], sums[1]).astype(jnp.bfloat16)
    got = swapped(sent, "z_hi")
    weight_gradient = kept + got.astype(jnp.float32)

    *local, tail = backward(here, segments, queries, keys, values, gradient, head_output, chances)
    arrived = swapped(tail, "z_hi")
    local = settle(here, counts, local, arrived)
    return (*local, weight_gradient)


def solution(mesh):
    split = Mesh(mesh.devices.reshape(2, 4, 4, CHIPS, 2), AXES)
    placed = (
        P(DP, TENSOR),
        P(DP, TENSOR),
        P(DP, TENSOR),
        P(AXES, None),
        P(TENSOR, None),
        P(),
        P(),
    )
    return jax.shard_map(
        steps,
        mesh=split,
        in_specs=placed,
        out_specs=(P(DP, TENSOR), P(DP, TENSOR), P(DP, TENSOR), P(DP, TENSOR)),
        check_vma=False,
    )
```

profile of v0, /device:TPU:1, one launch (start us, length us, event | category | flops | bytes accessed | tf_op | source)
XLA Modules:
  0.0 223.1 jit_solution(15415758284366612373)
XLA Ops:
  2.1 2.5 %collective-permute-start.1 = (bf16[128,2560]{1,0:T(8,128)(2,1)S(1)}, bf16[128,2560]{1,0:T(8,128)(2,1)}, u32[]{:S(2)}, u32[]{:S(2)}) collective-permute-start(bf16[128,2560]{1,0:T(8,128)(2,1)S(1)} %get-tuple-element.26), channel_id=1, source_target_pairs={{0,2},{2,4},{4,6},{6,0},{1,3},{3,5},{5,7},{7,1},{8,10},{10,12},{12... | collective-permute-start | bytes 1966088 | tf_op jit(solution)/shard_map/ppermute | solution.py:317
  4.7 16.3 %collective-permute-done.1.refs_2_ = bf16[128,2560]{1,0:T(8,128)(2,1)} collective-permute-done((bf16[128,2560]{1,0:T(8,128)(2,1)S(1)}, bf16[128,2560]{1,0:T(8,128)(2,1)}, u32[]{:S(2)}, u32[]{:S(2)}) %collective-permute-start.1) | collective-permute-done | bytes 655392 | tf_op jit(solution)/shard_map/ppermute | solution.py:317
  21.0 2.2 collective-permute-start
  23.2 14.1 %collective-permute-done.2.refs_4_ = bf16[128,2560]{1,0:T(8,128)(2,1)} collective-permute-done((bf16[128,2560]{1,0:T(8,128)(2,1)}, bf16[128,2560]{1,0:T(8,128)(2,1)}, u32[]{:S(2)}, u32[]{:S(2)}) %collective-permute-start.2) | collective-permute-done | bytes 655392 | tf_op jit(solution)/shard_map/ppermute | solution.py:317
  37.3 3.0 %collective-permute-start.9 = (bf16[128,2560]{1,0:T(8,128)(2,1)}, bf16[128,2560]{1,0:T(8,128)(2,1)}, u32[]{:S(2)}, u32[]{:S(2)}) collective-permute-start(bf16[128,2560]{1,0:T(8,128)(2,1)} %collective-permute-done.1.refs_2_), channel_id=1, source_target_pairs={{0,1},{1,0},{2,3},{3,2},{4,5},{5,4},{6,7},{7,6},{8,9},{9,8},{10,11... | collective-permute-start | bytes 1966088 | tf_op jit(solution)/shard_map/ppermute | solution.py:29
  40.4 12.3 %collective-permute-done.11.refs_6_ = bf16[128,2560]{1,0:T(8,128)(2,1)} collective-permute-done((bf16[128,2560]{1,0:T(8,128)(2,1)}, bf16[128,2560]{1,0:T(8,128)(2,1)}, u32[]{:S(2)}, u32[]{:S(2)}) %collective-permute-start.11) | collective-permute-done | bytes 655392 | tf_op jit(solution)/shard_map/ppermute | solution.py:317
  52.6 7.3 %collective-permute-start.12 = (bf16[128,2560]{1,0:T(8,128)(2,1)}, bf16[128,2560]{1,0:T(8,128)(2,1)}, u32[]{:S(2)}, u32[]{:S(2)}) collective-permute-start(bf16[128,2560]{1,0:T(8,128)(2,1)} %collective-permute-done.11.refs_6_), channel_id=1, source_target_pairs={{0,1},{1,0},{2,3},{3,2},{4,5},{5,4},{6,7},{7,6},{8,9},{9,8},{10,11... | collective-permute-start | bytes 1966088 | tf_op jit(solution)/shard_map/ppermute | solution.py:29
  60.0 6.7 %collective-permute-done.3.refs_2_ = bf16[128,2560]{1,0:T(8,128)(2,1)} collective-permute-done((bf16[128,2560]{1,0:T(8,128)(2,1)S(1)}, bf16[128,2560]{1,0:T(8,128)(2,1)}, u32[]{:S(2)}, u32[]{:S(2)}) %collective-permute-start.3) | collective-permute-done | bytes 655392 | tf_op jit(solution)/shard_map/ppermute | solution.py:317
  70.3 10.3 %forward.1 = (bf16[3,1024,512]{2,1,0:T(8,128)(2,1)S(1)}, bf16[1024,384]{1,0:T(8,128)(2,1)S(1)}, bf16[1024,384]{1,0:T(8,128)(2,1)S(1)}) custom-call(s32[3]{0:T(128)S(1)} %pad_add_fusion.here_ref, s32[32,8]{1,0:T(8,128)S(1)} %copy.15.ids_ref, bf16[1024,384]{1,0:T(8,128)(2,1)S(1)} %copy-done.15, bf16[1024,384]{1,0:T(8,128)(2,1)S(1)} %copy-done.17, ...), custom_call_target="tpu_custom_call" | custom-call | flops 805306368 | bytes 7077888 | tf_op jit(solution)/shard_map/forward/pallas_call | solution.py:155
  83.1 5.2 %weight.3 = bf16[2560,384]{1,0:T(8,128)(2,1)S(1)} custom-call(s32[3]{0:T(128)S(1)} %pad_add_fusion.here_ref, bf16[128,5120]{1,0:T(8,128)(2,1)S(1)} %copy-done, bf16[128,5120]{1,0:T(8,128)(2,1)S(1)} %collective-permute-done.refs_1_, bf16[128,2560]{1,0:T(8,128)(2,1)} %collective-permute-done.1.refs_2_, bf16[128,2560]{1,0:T(8,128)(2,1)} %collective-permute-done.9.refs_3_, ...), custom_call_target="tpu_custom_call" | custom-call | flops 2013265920 | bytes 7995392 | tf_op jit(solution)/shard_map/weight/pallas_call | solution.py:284
  89.7 9.5 %all-to-all-start.1 = ((bf16[16,160,384]{2,1,0:T(8,128)(2,1)}), bf16[16,160,384]{2,1,0:T(8,128)(2,1)}, u32[]{:S(2)}, u32[]{:S(2)}) async-start(bf16[16,160,384]{2,1,0:T(8,128)(2,1)} %bitcast.6), calls=%async_computation.1 | async-start | bytes 3932160 | tf_op jit(solution)/shard_map/all_to_all | solution.py:339
  99.3 3.3 %collective-permute-start.4 = (bf16[128,2560]{1,0:T(8,128)(2,1)}, bf16[128,2560]{1,0:T(8,128)(2,1)S(1)}, u32[]{:S(2)}, u32[]{:S(2)}) collective-permute-start(bf16[128,2560]{1,0:T(8,128)(2,1)} %collective-permute-done.3.refs_2_), channel_id=1, source_target_pairs={{0,1},{1,0},{2,3},{3,2},{4,5},{5,4},{6,7},{7,6},{8,9},{9,8},{10,11... | collective-permute-start | bytes 1966088 | tf_op jit(solution)/shard_map/ppermute | solution.py:29
  102.8 11.7 %collective-permute-done.7.refs_6_ = bf16[128,2560]{1,0:T(8,128)(2,1)S(1)} collective-permute-done((bf16[128,2560]{1,0:T(8,128)(2,1)}, bf16[128,2560]{1,0:T(8,128)(2,1)S(1)}, u32[]{:S(2)}, u32[]{:S(2)}) %collective-permute-start.7) | collective-permute-done | bytes 655392 | tf_op jit(solution)/shard_map/ppermute | solution.py:317
  114.5 4.0 %collective-permute-start.8 = (bf16[128,2560]{1,0:T(8,128)(2,1)S(1)}, bf16[128,2560]{1,0:T(8,128)(2,1)S(1)}, u32[]{:S(2)}, u32[]{:S(2)}) collective-permute-start(bf16[128,2560]{1,0:T(8,128)(2,1)S(1)} %collective-permute-done.7.refs_6_), channel_id=1, source_target_pairs={{0,1},{1,0},{2,3},{3,2},{4,5},{5,4},{6,7},{7,6},{8,9},{9,8},{10,11... | collective-permute-start | bytes 1966088 | tf_op jit(solution)/shard_map/ppermute | solution.py:29
  120.2 4.8 %weight.2 = bf16[2560,384]{1,0:T(8,128)(2,1)S(1)} custom-call(s32[3]{0:T(128)S(1)} %pad_add_fusion.here_ref, bf16[128,5120]{1,0:T(8,128)(2,1)S(1)} %copy-done, bf16[128,5120]{1,0:T(8,128)(2,1)S(1)} %collective-permute-done.refs_1_, bf16[128,2560]{1,0:T(8,128)(2,1)} %collective-permute-done.3.refs_2_, bf16[128,2560]{1,0:T(8,128)(2,1)S(1)} %collective-permute-done.4.refs_3_, ...), custom_call_target="tpu_custom_call" | custom-call | flops 2013265920 | bytes 7995392 | tf_op jit(solution)/shard_map/weight/pallas_call | solution.py:284
  129.7 6.7 %all-to-all-start = ((bf16[16,160,384]{2,1,0:T(8,128)(2,1)}), bf16[16,160,384]{2,1,0:T(8,128)(2,1)}, u32[]{:S(2)}, u32[]{:S(2)}) async-start(bf16[16,160,384]{2,1,0:T(8,128)(2,1)} %bitcast.5), calls=%async_computation | async-start | bytes 3932160 | tf_op jit(solution)/shard_map/all_to_all | solution.py:339
  136.4 2.1 copy-done.1
  138.5 5.8 %project.2.refs_9_ = f32[1024,384]{1,0:T(8,128)S(1)} custom-call(s32[3]{0:T(128)S(1)} %pad_add_fusion.here_ref, bf16[128,5120]{1,0:T(8,128)(2,1)S(1)} %copy-done, bf16[128,5120]{1,0:T(8,128)(2,1)S(1)} %collective-permute-done.refs_1_, bf16[128,2560]{1,0:T(8,128)(2,1)} %collective-permute-done.1.refs_2_, bf16[128,2560]{1,0:T(8,128)(2,1)} %collective-permute-done.9.refs_3_, ...), custom_call_target="tpu_custom_call" | custom-call | flops 2013265920 | bytes 10354688 | tf_op jit(solution)/shard_map/project/pallas_call | solution.py:259
  144.5 5.5 %project.3.g_ref = bf16[1024,384]{1,0:T(8,128)(2,1)S(1)} custom-call(s32[3]{0:T(128)S(1)} %pad_add_fusion.here_ref, bf16[128,5120]{1,0:T(8,128)(2,1)S(1)} %copy-done, bf16[128,5120]{1,0:T(8,128)(2,1)S(1)} %collective-permute-done.refs_1_, bf16[128,2560]{1,0:T(8,128)(2,1)} %collective-permute-done.3.refs_2_, bf16[128,2560]{1,0:T(8,128)(2,1)S(1)} %copy-done.10, ...), custom_call_target="tpu_custom_call" | custom-call | flops 2013265920 | bytes 10354688 | tf_op jit(solution)/shard_map/project/pallas_call | solution.py:259
  150.1 10.4 %backward.1 = (bf16[1024,384]{1,0:T(8,128)(2,1)}, bf16[1024,384]{1,0:T(8,128)(2,1)}, bf16[1024,384]{1,0:T(8,128)(2,1)}, bf16[3,512,384]{2,1,0:T(8,128)(2,1)S(1)}) custom-call(s32[3]{0:T(128)S(1)} %pad_add_fusion.here_ref, s32[32,8]{1,0:T(8,128)S(1)} %copy.15.ids_ref, bf16[1024,384]{1,0:T(8,128)(2,1)S(1)} %copy-done.16, bf16[1024,384]{1,0:T(8,128)(2,1)S(1)} %copy-done.18, ...), custom_call_target="tpu_custom_call" | custom-call | flops 1610612736 | bytes 10616832 | tf_op jit(solution)/shard_map/backward/pallas_call | solution.py:177
  160.5 5.0 %collective-permute-start.13 = (bf16[3,512,384]{2,1,0:T(8,128)(2,1)S(1)}, bf16[3,512,384]{2,1,0:T(8,128)(2,1)S(1)}, u32[]{:S(2)}, u32[]{:S(2)}) collective-permute-start(bf16[3,512,384]{2,1,0:T(8,128)(2,1)S(1)} %get-tuple-element.21), channel_id=1, source_target_pairs={{0,128},{128,0},{1,129},{129,1},{2,130},{130,2},{3,131},{131,3},{4... | collective-permute-start | bytes 3538952 | tf_op jit(solution)/shard_map/ppermute | solution.py:29
  167.4 1.8 convert_reduce_fusion.1
  169.2 4.1 %collective-permute-start.14 = (bf16[160,384]{1,0:T(8,128)(2,1)S(1)}, bf16[160,384]{1,0:T(8,128)(2,1)S(1)}, u32[]{:S(2)}, u32[]{:S(2)}) collective-permute-start(bf16[160,384]{1,0:T(8,128)(2,1)S(1)} %select_convert_fusion), channel_id=1, source_target_pairs={{0,128},{128,0},{1,129},{129,1},{2,130},{130,2},{3,131},{131,3},{4... | collective-permute-start | bytes 368648 | tf_op jit(solution)/shard_map/ppermute | solution.py:29
  173.3 46.4 %collective-permute-done.13.refs_3_ = bf16[3,512,384]{2,1,0:T(8,128)(2,1)S(1)} collective-permute-done((bf16[3,512,384]{2,1,0:T(8,128)(2,1)S(1)}, bf16[3,512,384]{2,1,0:T(8,128)(2,1)S(1)}, u32[]{:S(2)}, u32[]{:S(2)}) %collective-permute-start.13) | collective-permute-done | bytes 1179680 | tf_op jit(solution)/shard_map/ppermute | solution.py:29
  (74 shorter events, 20.8 us)
Async XLA Ops:
  0.6 20.4 %copy-start = (bf16[128,5120]{1,0:T(8,128)(2,1)S(1)}, bf16[128,5120]{1,0:T(8,128)(2,1)}, u32[]{:S(2)}) copy-start(bf16[128,5120]{1,0:T(8,128)(2,1)} %refs_0_.7) | copy-start | bytes 3932164
  0.6 66.1 %copy-start.24 = (s32[32,8]{0,1:T(8,128)S(1)}, s32[32,8]{0,1:T(8,128)}, u32[]{:S(2)}) copy-start(s32[32,8]{0,1:T(8,128)} %param.12) | copy-start | bytes 3076
  2.1 18.9 %collective-permute-start.1 = (bf16[128,2560]{1,0:T(8,128)(2,1)S(1)}, bf16[128,2560]{1,0:T(8,128)(2,1)}, u32[]{:S(2)}, u32[]{:S(2)}) collective-permute-start(bf16[128,2560]{1,0:T(8,128)(2,1)S(1)} %get-tuple-element.26), channel_id=1, source_target_pairs={{0,2},{2,4},{4,6},{6,0},{1,3},{3,5},{5,7},{7,1},{8,10},{10,12},{12... | collective-permute-start | bytes 1966088 | tf_op jit(solution)/shard_map/ppermute | solution.py:317
  21.0 16.2 %collective-permute-start.2 = (bf16[128,2560]{1,0:T(8,128)(2,1)}, bf16[128,2560]{1,0:T(8,128)(2,1)}, u32[]{:S(2)}, u32[]{:S(2)}) collective-permute-start(bf16[128,2560]{1,0:T(8,128)(2,1)} %collective-permute-done.1.refs_2_), channel_id=1, source_target_pairs={{0,2},{2,4},{4,6},{6,0},{1,3},{3,5},{5,7},{7,1},{8,10},{10,12},{12... | collective-permute-start | bytes 1966088 | tf_op jit(solution)/shard_map/ppermute | solution.py:317
  21.0 62.1 %collective-permute-start = (bf16[128,5120]{1,0:T(8,128)(2,1)S(1)}, bf16[128,5120]{1,0:T(8,128)(2,1)S(1)}, u32[]{:S(2)}, u32[]{:S(2)}) collective-permute-start(bf16[128,5120]{1,0:T(8,128)(2,1)S(1)} %copy-done), channel_id=1, source_target_pairs={{0,1},{1,0},{2,3},{3,2},{4,5},{5,4},{6,7},{7,6},{8,9},{9,8},{10,11... | collective-permute-start | bytes 3932168 | tf_op jit(solution)/shard_map/ppermute | solution.py:29
  37.3 15.4 %collective-permute-start.11 = (bf16[128,2560]{1,0:T(8,128)(2,1)}, bf16[128,2560]{1,0:T(8,128)(2,1)}, u32[]{:S(2)}, u32[]{:S(2)}) collective-permute-start(bf16[128,2560]{1,0:T(8,128)(2,1)} %collective-permute-done.2.refs_4_), channel_id=1, source_target_pairs={{0,2},{2,4},{4,6},{6,0},{1,3},{3,5},{5,7},{7,1},{8,10},{10,12},{12... | collective-permute-start | bytes 1966088 | tf_op jit(solution)/shard_map/ppermute | solution.py:317
  37.3 29.4 %collective-permute-start.3 = (bf16[128,2560]{1,0:T(8,128)(2,1)S(1)}, bf16[128,2560]{1,0:T(8,128)(2,1)}, u32[]{:S(2)}, u32[]{:S(2)}) collective-permute-start(bf16[128,2560]{1,0:T(8,128)(2,1)S(1)} %get-tuple-element.15), channel_id=1, source_target_pairs={{0,2},{2,4},{4,6},{6,0},{1,3},{3,5},{5,7},{7,1},{8,10},{10,12},{12... | collective-permute-start | bytes 1966088 | tf_op jit(solution)/shard_map/ppermute | solution.py:317
  37.3 45.8 %collective-permute-start.9 = (bf16[128,2560]{1,0:T(8,128)(2,1)}, bf16[128,2560]{1,0:T(8,128)(2,1)}, u32[]{:S(2)}, u32[]{:S(2)}) collective-permute-start(bf16[128,2560]{1,0:T(8,128)(2,1)} %collective-permute-done.1.refs_2_), channel_id=1, source_target_pairs={{0,1},{1,0},{2,3},{3,2},{4,5},{5,4},{6,7},{7,6},{8,9},{9,8},{10,11... | collective-permute-start | bytes 1966088 | tf_op jit(solution)/shard_map/ppermute | solution.py:29
  40.3 42.8 %collective-permute-start.10 = (bf16[128,2560]{1,0:T(8,128)(2,1)}, bf16[128,2560]{1,0:T(8,128)(2,1)}, u32[]{:S(2)}, u32[]{:S(2)}) collective-permute-start(bf16[128,2560]{1,0:T(8,128)(2,1)} %collective-permute-done.2.refs_4_), channel_id=1, source_target_pairs={{0,1},{1,0},{2,3},{3,2},{4,5},{5,4},{6,7},{7,6},{8,9},{9,8},{10,11... | collective-permute-start | bytes 1966088 | tf_op jit(solution)/shard_map/ppermute | solution.py:29
  52.6 30.5 %collective-permute-start.12 = (bf16[128,2560]{1,0:T(8,128)(2,1)}, bf16[128,2560]{1,0:T(8,128)(2,1)}, u32[]{:S(2)}, u32[]{:S(2)}) collective-permute-start(bf16[128,2560]{1,0:T(8,128)(2,1)} %collective-permute-done.11.refs_6_), channel_id=1, source_target_pairs={{0,1},{1,0},{2,3},{3,2},{4,5},{5,4},{6,7},{7,6},{8,9},{9,8},{10,11... | collective-permute-start | bytes 1966088 | tf_op jit(solution)/shard_map/ppermute | solution.py:29
  66.7 32.5 %collective-permute-start.5 = (bf16[128,2560]{1,0:T(8,128)(2,1)}, bf16[128,2560]{1,0:T(8,128)(2,1)}, u32[]{:S(2)}, u32[]{:S(2)}) collective-permute-start(bf16[128,2560]{1,0:T(8,128)(2,1)} %collective-permute-done.3.refs_2_), channel_id=1, source_target_pairs={{0,2},{2,4},{4,6},{6,0},{1,3},{3,5},{5,7},{7,1},{8,10},{10,12},{12... | collective-permute-start | bytes 1966088 | tf_op jit(solution)/shard_map/ppermute | solution.py:317
  89.7 40.0 %all-to-all-start.1 = ((bf16[16,160,384]{2,1,0:T(8,128)(2,1)}), bf16[16,160,384]{2,1,0:T(8,128)(2,1)}, u32[]{:S(2)}, u32[]{:S(2)}) async-start(bf16[16,160,384]{2,1,0:T(8,128)(2,1)} %bitcast.6), calls=%async_computation.1 | async-start | bytes 3932160 | tf_op jit(solution)/shard_map/all_to_all | solution.py:339
  99.2 15.2 %collective-permute-start.7 = (bf16[128,2560]{1,0:T(8,128)(2,1)}, bf16[128,2560]{1,0:T(8,128)(2,1)S(1)}, u32[]{:S(2)}, u32[]{:S(2)}) collective-permute-start(bf16[128,2560]{1,0:T(8,128)(2,1)} %collective-permute-done.5.refs_4_), channel_id=1, source_target_pairs={{0,2},{2,4},{4,6},{6,0},{1,3},{3,5},{5,7},{7,1},{8,10},{10,12},{12... | collective-permute-start | bytes 1966088 | tf_op jit(solution)/shard_map/ppermute | solution.py:317
  99.3 19.2 %collective-permute-start.4 = (bf16[128,2560]{1,0:T(8,128)(2,1)}, bf16[128,2560]{1,0:T(8,128)(2,1)S(1)}, u32[]{:S(2)}, u32[]{:S(2)}) collective-permute-start(bf16[128,2560]{1,0:T(8,128)(2,1)} %collective-permute-done.3.refs_2_), channel_id=1, source_target_pairs={{0,1},{1,0},{2,3},{3,2},{4,5},{5,4},{6,7},{7,6},{8,9},{9,8},{10,11... | collective-permute-start | bytes 1966088 | tf_op jit(solution)/shard_map/ppermute | solution.py:29
  102.7 15.8 %collective-permute-start.6 = (bf16[128,2560]{1,0:T(8,128)(2,1)}, bf16[128,2560]{1,0:T(8,128)(2,1)S(1)}, u32[]{:S(2)}, u32[]{:S(2)}) collective-permute-start(bf16[128,2560]{1,0:T(8,128)(2,1)} %collective-permute-done.5.refs_4_), channel_id=1, source_target_pairs={{0,1},{1,0},{2,3},{3,2},{4,5},{5,4},{6,7},{7,6},{8,9},{9,8},{10,11... | collective-permute-start | bytes 1966088 | tf_op jit(solution)/shard_map/ppermute | solution.py:29
  114.5 5.7 %collective-permute-start.8 = (bf16[128,2560]{1,0:T(8,128)(2,1)S(1)}, bf16[128,2560]{1,0:T(8,128)(2,1)S(1)}, u32[]{:S(2)}, u32[]{:S(2)}) collective-permute-start(bf16[128,2560]{1,0:T(8,128)(2,1)S(1)} %collective-permute-done.7.refs_6_), channel_id=1, source_target_pairs={{0,1},{1,0},{2,3},{3,2},{4,5},{5,4},{6,7},{7,6},{8,9},{9,8},{10,11... | collective-permute-start | bytes 1966088 | tf_op jit(solution)/shard_map/ppermute | solution.py:29
  129.7 37.6 %all-to-all-start = ((bf16[16,160,384]{2,1,0:T(8,128)(2,1)}), bf16[16,160,384]{2,1,0:T(8,128)(2,1)}, u32[]{:S(2)}, u32[]{:S(2)}) async-start(bf16[16,160,384]{2,1,0:T(8,128)(2,1)} %bitcast.5), calls=%async_computation | async-start | bytes 3932160 | tf_op jit(solution)/shard_map/all_to_all | solution.py:339
  138.5 5.9 %copy-start.8 = (bf16[128,2560]{1,0:T(8,128)(2,1)S(1)}, bf16[128,2560]{1,0:T(8,128)(2,1)}, u32[]{:S(2)}) copy-start(bf16[128,2560]{1,0:T(8,128)(2,1)} %copy-done.7) | copy-start | bytes 1966084
  138.5 5.9 %copy-start.10 = (bf16[128,2560]{1,0:T(8,128)(2,1)S(1)}, bf16[128,2560]{1,0:T(8,128)(2,1)}, u32[]{:S(2)}) copy-start(bf16[128,2560]{1,0:T(8,128)(2,1)} %copy-done.9) | copy-start | bytes 1966084
  138.5 5.9 %copy-start.12 = (bf16[128,2560]{1,0:T(8,128)(2,1)S(1)}, bf16[128,2560]{1,0:T(8,128)(2,1)}, u32[]{:S(2)}) copy-start(bf16[128,2560]{1,0:T(8,128)(2,1)} %copy-done.11) | copy-start | bytes 1966084
  138.5 5.9 %copy-start.14 = (bf16[128,2560]{1,0:T(8,128)(2,1)S(1)}, bf16[128,2560]{1,0:T(8,128)(2,1)}, u32[]{:S(2)}) copy-start(bf16[128,2560]{1,0:T(8,128)(2,1)} %copy-done.13) | copy-start | bytes 1966084
  160.5 59.3 %collective-permute-start.13 = (bf16[3,512,384]{2,1,0:T(8,128)(2,1)S(1)}, bf16[3,512,384]{2,1,0:T(8,128)(2,1)S(1)}, u32[]{:S(2)}, u32[]{:S(2)}) collective-permute-start(bf16[3,512,384]{2,1,0:T(8,128)(2,1)S(1)} %get-tuple-element.21), channel_id=1, source_target_pairs={{0,128},{128,0},{1,129},{129,1},{2,130},{130,2},{3,131},{131,3},{4... | collective-permute-start | bytes 3538952 | tf_op jit(solution)/shard_map/ppermute | solution.py:29
  167.3 52.4 %copy-start.23 = (s32[32]{0:T(128)S(1)}, s32[32]{0:T(128)}, u32[]{:S(2)}) copy-start(s32[32]{0:T(128)} %counts_ref.1) | copy-start | bytes 388
  169.2 53.2 %collective-permute-start.14 = (bf16[160,384]{1,0:T(8,128)(2,1)S(1)}, bf16[160,384]{1,0:T(8,128)(2,1)S(1)}, u32[]{:S(2)}, u32[]{:S(2)}) collective-permute-start(bf16[160,384]{1,0:T(8,128)(2,1)S(1)} %select_convert_fusion), channel_id=1, source_target_pairs={{0,128},{128,0},{1,129},{129,1},{2,130},{130,2},{3,131},{131,3},{4... | collective-permute-start | bytes 368648 | tf_op jit(solution)/shard_map/ppermute | solution.py:29
  (18 other events, 48.0 us)
where the time goes:
time: 224 us; the launch traced here: 223 us
  waiting for transfers between devices  110 us (49%)
  starting transfers between devices  47.9 us (21%)
  Pallas kernels  43.9 us (20%)
  local copies, waits for them, and re-layouts  15.6 us (7%)
  other arithmetic  4.53 us (2%)
    ppermute x6, waiting for transfers between devices, turn(): y = lax.ppermute(x, 'z_lo', ring)  61.1 us
    ppermute x9, waiting for transfers between devices, swapped(): return lax.ppermute(x, axis, [(i, (i + n // 2) % n) for i in range(n)])  49.1 us
    ppermute x9, starting transfers between devices, swapped(): return lax.ppermute(x, axis, [(i, (i + n // 2) % n) for i in range(n)])  29.1 us
    all_to_all x2, starting transfers between devices, steps(): tiles = lax.all_to_all(tiles, ('y', 'x'), 0, 0, tiled=True)  16.2 us
    unnamed x51, local copies, waits for them, and re-layouts  14.1 us
    pallas_call x2, Pallas kernels, project(): pl.pallas_call(functools.partial(project_kernel, last), grid_spec=prefetc...  11.4 us
    pallas_call x1, Pallas kernels, backward(): pl.pallas_call(backward_kernel, grid_spec=prefetched(2, (heads,), [hs] *...  10.4 us
    pallas_call x1, Pallas kernels, forward(): pl.pallas_call(forward_kernel, grid_spec=prefetched(2, (heads,), [hs] * 3...  10.3 us
  transfers between devices with their start and end apart: 17, of which 8 were waited for; matrix products, arithmetic and copies ran while one was open for 2% of the time, Pallas kernels for 20%

commit v1 on v0

--- a/solution.py
+++ b/solution.py
@@ -53,30 +53,32 @@
     return own, start, pl.ds(pl.multiple_of(start * BLOCK, BLOCK), WINDOW * BLOCK)
 
 
-def forward_kernel(here_ref, ids_ref, q_ref, k_ref, v_ref, p_ref, o_ref, r_ref):
+def forward_kernel(here_ref, ids_ref, q_ref, k_ref, v_ref, p_ref, o_ref, r_ref, kt_ref, vt):
     row, chip, core = here_ref[0], here_ref[1], here_ref[2]
+    kt_ref[...] = k_ref[...].T
+    vt[...] = v_ref[...].T
     for b in range(ids_ref.shape[1]):
         own, start, near = window_of(ids_ref, row, b)
         rows = pl.ds(b * BLOCK, BLOCK)
-        scores = dot(q_ref[rows, :], k_ref[near, :], (1, 1))
+        scores = dot(k_ref[near, :], q_ref[rows, :], (1, 1))
         tiles = []
         for t in range(WINDOW):
             off = jnp.where(ids_ref[row, start + t] == own, 0.0, masked_score)
-            tiles.append(scores[:, t * BLOCK : (t + 1) * BLOCK] + off)
-        top = jnp.max(functools.reduce(jnp.maximum, tiles), axis=1, keepdims=True)
+            tiles.append(scores[t * BLOCK : (t + 1) * BLOCK] + off)
+        top = jnp.max(functools.reduce(jnp.maximum, tiles), axis=0, keepdims=True)
         tiles = [jnp.exp2((x - top) * (SCALE * LOG2E)) for x in tiles]
-        total = jnp.sum(functools.reduce(jnp.add, tiles), axis=1, keepdims=True)
+        total = jnp.sum(functools.reduce(jnp.add, tiles), axis=0, keepdims=True)
         inverse = 1.0 / total
-        p = jnp.concatenate([(x * inverse).astype(jnp.bfloat16) for x in tiles], axis=1)
-        p_ref[0, rows, :] = p
-        o = dot(p, v_ref[near, :], (1, 0)).astype(jnp.bfloat16)
+        p = jnp.concatenate([(x * inverse).astype(jnp.bfloat16) for x in tiles], axis=0)
+        p_ref[0, b] = p
+        o = dot(vt[:, near], p, (1, 0)).T.astype(jnp.bfloat16)
         o_ref[rows, :] = o
         turn = lax.rem(chip + CHIPS - b // 2, CHIPS)
         r_ref[block_at(2 * turn + jnp.where(core == b % 2, 0, 1)), :] = o
 
 
 def backward_kernel(
-    here_ref, ids_ref, q_ref, k_ref, v_ref, g_ref, o_ref, p_ref,
+    here_ref, ids_ref, q_ref, kt_ref, v_ref, g_ref, o_ref, p_ref,
     dq_ref, dk_ref, dv_ref, tail_ref, ka, va,
 ):
     row = here_ref[0]
@@ -87,15 +89,15 @@
         _, _, near = window_of(ids_ref, row, b)
         rows = pl.ds(b * BLOCK, BLOCK)
         g = g_ref[rows, :]
-        p = p_ref[0, rows, :]
-        dp = dot(g, v_ref[near, :], (1, 1))
+        p = p_ref[0, b]
+        dp = dot(v_ref[near, :], g, (1, 1))
         center = jnp.sum(
-            g.astype(jnp.float32) * o_ref[rows, :].astype(jnp.float32), axis=1, keepdims=True
+            (g.astype(jnp.float32) * o_ref[rows, :].astype(jnp.float32)).T, axis=0, keepdims=True
         )
         ds = (p.astype(jnp.float32) * (dp - center)).astype(jnp.bfloat16)
-        dq_ref[rows, :] = (dot(ds, k_ref[near, :], (1, 0)) * SCALE).astype(jnp.bfloat16)
-        ka[near, :] += dot(ds, q_ref[rows, :], (0, 0))
-        va[near, :] += dot(p, g, (0, 0))
+        dq_ref[rows, :] = (dot(kt_ref[:, near], ds, (1, 0)) * SCALE).T.astype(jnp.bfloat16)
+        ka[near, :] += dot(ds, q_ref[rows, :], (1, 0))
+        va[near, :] += dot(p, g, (1, 0))
     dk_ref[...] = (ka[...] * SCALE).astype(jnp.bfloat16)
     dv_ref[...] = va[...].astype(jnp.bfloat16)
     for i, ref in enumerate((dq_ref, dk_ref, dv_ref)):
@@ -148,38 +150,51 @@
 
 def forward(here, ids, q, k, v):
     rows, inner = q.shape
-    heads = inner // HEAD_SIZE
+    heads, blocks = inner // HEAD_SIZE, rows // BLOCK
     keys = WINDOW * BLOCK
     hs = pl.BlockSpec((rows, HEAD_SIZE), lambda h, *_: (0, h))
+    ps = pl.BlockSpec((1, blocks, keys, BLOCK), lambda h, *_: (h, 0, 0, 0))
+    ts = pl.BlockSpec((HEAD_SIZE, rows), lambda h, *_: (h, 0))
     out = jax.ShapeDtypeStruct((rows, inner), jnp.bfloat16)
     return pl.pallas_call(
         forward_kernel,
         grid_spec=prefetched(
-            2, (heads,), [hs] * 3, [pl.BlockSpec((1, rows, keys), lambda h, *_: (h, 0, 0)), hs, hs]
-        ),
-        out_shape=[jax.ShapeDtypeStruct((heads, rows, keys), jnp.bfloat16), out, out],
+            2,
+            (heads,),
+            [hs] * 3,
+            [ps, hs, hs, ts],
+            [pltpu.VMEM((HEAD_SIZE, rows), jnp.bfloat16)],
+        ),
+        out_shape=[
+            jax.ShapeDtypeStruct((heads, blocks, keys, BLOCK), jnp.bfloat16),
+            out,
+            out,
+            jax.ShapeDtypeStruct((inner, rows), jnp.bfloat16),
+        ],
+        compiler_params=room(20),
         cost_estimate=cost(
             4 * rows * keys * inner,
-            10 * rows * inner + 2 * heads * rows * keys,
+            12 * rows * inner + 2 * heads * rows * keys,
             heads * rows * keys,
         ),
-        compiler_params=room(20),
         name="forward",
     )(here, ids, q, k, v)
 
 
-def backward(here, ids, q, k, v, g, o, p):
+def backward(here, ids, q, kt, v, g, o, p):
     rows, inner = q.shape
-    heads = inner // HEAD_SIZE
+    heads, blocks = inner // HEAD_SIZE, rows // BLOCK
     keys = WINDOW * BLOCK
     moving = MOVABLE * BLOCK
     hs = pl.BlockSpec((rows, HEAD_SIZE), lambda h, *_: (0, h))
+    ps = pl.BlockSpec((1, blocks, keys, BLOCK), lambda h, *_: (h, 0, 0, 0))
+    ts = pl.BlockSpec((HEAD_SIZE, rows), lambda h, *_: (h, 0))
     return pl.pallas_call(
         backward_kernel,
         grid_spec=prefetched(
             2,
             (heads,),
-            [hs] * 5 + [pl.BlockSpec((1, rows, keys), lambda h, *_: (h, 0, 0))],
+            [hs, ts, hs, hs, hs, ps],
             [hs] * 3 + [pl.BlockSpec((3, moving, HEAD_SIZE), lambda h, *_: (0, 0, h))],
             [pltpu.VMEM((rows, HEAD_SIZE), jnp.float32)] * 2,
         ),
@@ -188,7 +203,7 @@
         compiler_params=room(20),
         cost_estimate=cost(8 * rows * keys * inner, 19 * rows * inner + 2 * heads * rows * keys),
         name="backward",
-    )(here, ids, q, k, v, g, o, p)
+    )(here, ids, q, kt, v, g, o, p)
 
 
 def settle(here, counts, local, arrived):
@@ -209,16 +224,16 @@
     )(here, counts, *local, arrived)
 
 
-def project_kernel(last, here_ref, *refs):
-    pieces, w_ref = refs[: 2 * CHIPS], refs[2 * CHIPS]
+def project_kernel(turns, final, here_ref, *refs):
+    count = 2 * len(turns)
+    pieces, w_ref = refs[:count], refs[count]
     out_ref, acc = refs[-2:]
     step = pl.program_id(0)
     part = dot(jnp.concatenate([ref[...] for ref in pieces], axis=0), w_ref[...], (1, 1))
-    chained = len(refs) == 2 * CHIPS + 4
 
     @pl.when(step == 0)
     def _():
-        acc[...] = refs[2 * CHIPS + 1][...] + part if chained else part
+        acc[...] = refs[count + 1][...] + part if final else part
 
     @pl.when(step > 0)
     def _():
@@ -226,46 +241,65 @@
 
     @pl.when(step == pl.num_programs(0) - 1)
     def _():
-        if not last:
+        if not final:
             out_ref[...] = acc[...]
             return
         chip, core = here_ref[1], here_ref[2]
-        for i in range(2 * CHIPS):
-            source = lax.rem(chip + CHIPS - i // 2, CHIPS)
-            block = 2 * source + (core if i % 2 == 0 else 1 - core)
+        for i in range(count):
+            block = core if i % 2 == 0 else 1 - core
+            if len(turns) > 1:
+                block += 2 * lax.rem(chip + CHIPS - turns[i // 2], CHIPS)
             out_ref[block_at(block), :] = acc[i * BLOCK : (i + 1) * BLOCK].astype(jnp.bfloat16)
 
 
 def piece_specs(pieces, first, width):
-    def spec(i):
-        at = first // width if i < 2 else 0
-        return pl.BlockSpec((pieces[i].shape[0], width), lambda j, *_: (0, at + j))
-
-    return [spec(i) for i in range(len(pieces))]
-
-
-def project(here, pieces, first, width, w, before, last):
-    depth = pieces[2].shape[1]
+    def spec(x):
+        at = first // width if x.shape[1] > pieces[-1].shape[1] else 0
+        return pl.BlockSpec((x.shape[0], width), lambda j, *_: (0, at + j))
+
+    return [spec(x) for x in pieces]
+
+
+def in_hbm(x):
+    return pltpu.with_memory_space_constraint(x, pltpu.HBM)
+
+
+def project(here, turns, pieces, first, width, w, partial, before):
+    pieces = [x for t in turns for x in pieces[2 * t : 2 * t + 2]]
+    depth = pieces[-1].shape[1]
     rows = sum(x.shape[0] for x in pieces)
     inner = w.shape[0]
-    at = first // width
-    whole = pl.BlockSpec((rows, inner), lambda j, *_: (0, 0))
+    at, place = first // width, turns[0] * 2 * BLOCK // rows
+    final = partial is not None
     in_specs = piece_specs(pieces, first, width)
     in_specs.append(pl.BlockSpec((inner, width), lambda j, *_: (0, at + j)))
-    operands = [*pieces, w]
+    operands = [*pieces, in_hbm(w)]
+    aliases = {}
+    total = rows
+    out_spec = pl.BlockSpec((rows, inner), lambda j, *_: (0, 0))
+    if final:
+        total = partial.shape[0]
+        in_specs.append(pl.BlockSpec((rows, inner), lambda j, *_: (place, 0)))
+        operands.append(partial)
+        out_spec = pl.BlockSpec((total, inner), lambda j, *_: (0, 0))
     if before is not None:
-        in_specs.append(whole)
+        in_specs.append(ANY)
         operands.append(before)
+        aliases = {len(operands): 0}
+        out_spec = pl.BlockSpec(
+            (rows, inner), lambda j, here: (lax.rem(here[1] + CHIPS - turns[0], CHIPS), 0)
+        )
     return pl.pallas_call(
-        functools.partial(project_kernel, last),
+        functools.partial(project_kernel, turns, final),
         grid_spec=prefetched(
-            1, (depth // width,), in_specs, whole, [pltpu.VMEM((rows, inner), jnp.float32)]
-        ),
-        out_shape=jax.ShapeDtypeStruct((rows, inner), jnp.bfloat16 if last else jnp.float32),
+            1, (depth // width,), in_specs, out_spec, [pltpu.VMEM((rows, inner), jnp.float32)]
+        ),
+        out_shape=jax.ShapeDtypeStruct((total, inner), jnp.bfloat16 if final else jnp.float32),
+        input_output_aliases=aliases,
+        compiler_params=room(30),
         cost_estimate=cost(
             2 * rows * depth * inner, 2 * rows * depth + 2 * inner * depth + 8 * rows * inner
         ),
-        compiler_params=room(30),
         name="project",
     )(here, *operands)
 
@@ -309,7 +343,6 @@
     here = here.astype(jnp.int32)
     ring = [(i, (i + 1) % CHIPS) for i in range(CHIPS)]
 
-    own = [lax.slice_in_dim(out_gradient, c * half, (c + 1) * half, axis=1) for c in range(2)]
     partner = swapped(out_gradient, "core")
     pieces = [[out_gradient, partner] for _ in range(2)]
 
@@ -319,18 +352,19 @@
         pieces[c] += [y, z]
         return y
 
-    first = turn(0, own[0])
+    first = turn(0, lax.slice_in_dim(out_gradient, 0, half, axis=1))
+    later = lax.slice_in_dim(after(out_gradient, first), half, depth, axis=1)
     second = turn(0, first)
     turn(0, second)
-    x = after(own[1], second)
+    x = after(later, second)
     for _ in range(3):
         x = turn(1, x)
 
-    chances, head_output, output_turned = forward(here, segments, queries, keys, values)
-
-    gradient = None
-    for c in range(2):
-        gradient = project(here, pieces[c], c * half, 1280, out_weight, gradient, c == 1)
+    chances, head_output, output_turned, keys_turned = forward(here, segments, queries, keys, values)
+
+    partial = project(here, (0, 1, 2, 3), pieces[0], 0, 1280, out_weight, None, None)
+    gradient = project(here, (0, 1, 2), pieces[1], half, 1280, out_weight, partial, None)
+    gradient = project(here, (3,), pieces[1], half, 1280, out_weight, partial, gradient)
 
     sums = []
     for c in range(2):
@@ -344,7 +378,9 @@
     got = swapped(sent, "z_hi")
     weight_gradient = kept + got.astype(jnp.float32)
 
-    *local, tail = backward(here, segments, queries, keys, values, gradient, head_output, chances)
+    *local, tail = backward(
+        here, segments, queries, keys_turned, values, gradient, head_output, chances
+    )
     arrived = swapped(tail, "z_hi")
     local = settle(here, counts, local, arrived)
     return (*local, weight_gradient)

time: 224 us -> 219 us (0.978)
  Pallas kernels: 43.9 us -> 40.6 us
    pallas_call x1, Pallas kernels: 10.3 us -> 6.08 us  [forward(): pl.pallas_call(forward_kernel, grid_spec=prefetched(2, (heads,), [hs] * 3...]
    unnamed x51 -> x49, local copies, waits for them, and re-layouts: 14.1 us -> 12.9 us
    pallas_call x3 -> x4, Pallas kernels: 21.8 us -> 22.8 us  [the longest x3 14 us: project(): pl.pallas_call(functools.partial(project_kernel, turns, final), grid_spec...]
  transfers between devices with their start and end apart: 17 -> 17, of which waited for: 8 -> 9; matrix products, arithmetic and copies ran while one was open for 2% -> 2% of each run, Pallas kernels for 20% -> 19%
where the time goes in v1:
time: 219 us; the launch traced here: 218 us
  waiting for transfers between devices  108 us (49%)
  starting transfers between devices  49 us (22%)
  Pallas kernels  40.6 us (19%)
  local copies, waits for them, and re-layouts  15.2 us (7%)
  other arithmetic  4.53 us (2%)
    ppermute x6, waiting for transfers between devices, turn(): y = lax.ppermute(x, 'z_lo', ring)  59.8 us
    ppermute x9, waiting for transfers between devices, swapped(): return lax.ppermute(x, axis, [(i, (i + n // 2) % n) for i in range(n)])  48 us
    ppermute x9, starting transfers between devices, swapped(): return lax.ppermute(x, axis, [(i, (i + n // 2) % n) for i in range(n)])  30.1 us
    all_to_all x2, starting transfers between devices, steps(): tiles = lax.all_to_all(tiles, ('y', 'x'), 0, 0, tiled=True)  16.2 us
    pallas_call x3, Pallas kernels, project(): pl.pallas_call(functools.partial(project_kernel, turns, final), grid_spec...  14 us
    unnamed x49, local copies, waits for them, and re-layouts  12.9 us
    pallas_call x2, Pallas kernels, weight(): pl.pallas_call(weight_kernel, grid_spec=prefetched(1, (depth // width,),...  10.1 us
    pallas_call x1, Pallas kernels, backward(): pl.pallas_call(backward_kernel, grid_spec=prefetched(2, (heads,), [hs, ts...  8.87 us
  transfers between devices with their start and end apart: 17, of which 9 were waited for; matrix products, arithmetic and copies ran while one was open for 2% of the time, Pallas kernels for 19%

profile of v1, /device:TPU:1, one launch (start us, length us, event | category | flops | bytes accessed | tf_op | source)
XLA Modules:
  0.0 218.3 jit_solution(11889067803160047557)
XLA Ops:
  1.8 2.5 %collective-permute-start = (bf16[128,2560]{1,0:T(8,128)(2,1)S(1)}, bf16[128,2560]{1,0:T(8,128)(2,1)}, u32[]{:S(2)}, u32[]{:S(2)}) collective-permute-start(bf16[128,2560]{1,0:T(8,128)(2,1)S(1)} %slice.6), channel_id=1, source_target_pairs={{0,2},{2,4},{4,6},{6,0},{1,3},{3,5},{5,7},{7,1},{8,10},{10,12},{12... | collective-permute-start | bytes 1966088 | tf_op jit(solution)/shard_map/ppermute | solution.py:350
  4.3 16.3 %collective-permute-done.refs_2_ = bf16[128,2560]{1,0:T(8,128)(2,1)} collective-permute-done((bf16[128,2560]{1,0:T(8,128)(2,1)S(1)}, bf16[128,2560]{1,0:T(8,128)(2,1)}, u32[]{:S(2)}, u32[]{:S(2)}) %collective-permute-start) | collective-permute-done | bytes 655392 | tf_op jit(solution)/shard_map/ppermute | solution.py:350
  20.7 2.2 collective-permute-start.6
  22.8 14.1 %collective-permute-done.1.refs_4_ = bf16[128,2560]{1,0:T(8,128)(2,1)} collective-permute-done((bf16[128,2560]{1,0:T(8,128)(2,1)}, bf16[128,2560]{1,0:T(8,128)(2,1)}, u32[]{:S(2)}, u32[]{:S(2)}) %collective-permute-start.1) | collective-permute-done | bytes 655392 | tf_op jit(solution)/shard_map/ppermute | solution.py:350
  38.1 3.1 %collective-permute-start.7 = (bf16[128,2560]{1,0:T(8,128)(2,1)}, bf16[128,2560]{1,0:T(8,128)(2,1)}, u32[]{:S(2)}, u32[]{:S(2)}) collective-permute-start(bf16[128,2560]{1,0:T(8,128)(2,1)} %collective-permute-done.refs_2_), channel_id=1, source_target_pairs={{0,1},{1,0},{2,3},{3,2},{4,5},{5,4},{6,7},{7,6},{8,9},{9,8},{10,11... | collective-permute-start | bytes 1966088 | tf_op jit(solution)/shard_map/ppermute | solution.py:29
  41.4 11.0 %collective-permute-done.9.refs_6_ = bf16[128,2560]{1,0:T(8,128)(2,1)} collective-permute-done((bf16[128,2560]{1,0:T(8,128)(2,1)}, bf16[128,2560]{1,0:T(8,128)(2,1)}, u32[]{:S(2)}, u32[]{:S(2)}) %collective-permute-start.9) | collective-permute-done | bytes 655392 | tf_op jit(solution)/shard_map/ppermute | solution.py:350
  52.3 7.3 %collective-permute-start.10 = (bf16[128,2560]{1,0:T(8,128)(2,1)}, bf16[128,2560]{1,0:T(8,128)(2,1)}, u32[]{:S(2)}, u32[]{:S(2)}) collective-permute-start(bf16[128,2560]{1,0:T(8,128)(2,1)} %collective-permute-done.9.refs_6_), channel_id=1, source_target_pairs={{0,1},{1,0},{2,3},{3,2},{4,5},{5,4},{6,7},{7,6},{8,9},{9,8},{10,11... | collective-permute-start | bytes 1966088 | tf_op jit(solution)/shard_map/ppermute | solution.py:29
  59.6 6.7 %collective-permute-done.2.refs_2_ = bf16[128,2560]{1,0:T(8,128)(2,1)} collective-permute-done((bf16[128,2560]{1,0:T(8,128)(2,1)S(1)}, bf16[128,2560]{1,0:T(8,128)(2,1)}, u32[]{:S(2)}, u32[]{:S(2)}) %collective-permute-start.2) | collective-permute-done | bytes 655392 | tf_op jit(solution)/shard_map/ppermute | solution.py:350
  69.9 6.1 %forward.1 = (bf16[3,8,512,128]{3,2,1,0:T(8,128)(2,1)S(1)}, bf16[1024,384]{1,0:T(8,128)(2,1)S(1)}, bf16[1024,384]{1,0:T(8,128)(2,1)S(1)}, bf16[384,1024]{1,0:T(8,128)(2,1)S(1)}) custom-call(s32[3]{0:T(128)S(1)} %pad_add_fusion.here_ref, s32[32,8]{1,0:T(8,128)S(1)} %copy.16.ids_ref, bf16[1024,384]{1,0:T(8,128)(2,1)S(1)} %copy-done.13, ...), custom_call_target="tpu_custom_call" | custom-call | flops 805306368 | bytes 7864320 | tf_op jit(solution)/shard_map/forward/pallas_call | solution.py:159
  79.4 5.2 %weight.3 = bf16[2560,384]{1,0:T(8,128)(2,1)S(1)} custom-call(s32[3]{0:T(128)S(1)} %pad_add_fusion.here_ref, bf16[128,5120]{1,0:T(8,128)(2,1)S(1)} %copy-done, bf16[128,5120]{1,0:T(8,128)(2,1)S(1)} %collective-permute-done.6.refs_1_, bf16[128,2560]{1,0:T(8,128)(2,1)} %collective-permute-done.refs_2_, bf16[128,2560]{1,0:T(8,128)(2,1)} %collective-permute-done.7.refs_3_, ...), custom_call_target="tpu_custom_call" | custom-call | flops 2013265920 | bytes 7995392 | tf_op jit(solution)/shard_map/weight/pallas_call | solution.py:318
  86.0 9.5 %all-to-all-start.1 = ((bf16[16,160,384]{2,1,0:T(8,128)(2,1)}), bf16[16,160,384]{2,1,0:T(8,128)(2,1)}, u32[]{:S(2)}, u32[]{:S(2)}) async-start(bf16[16,160,384]{2,1,0:T(8,128)(2,1)} %bitcast.6), calls=%async_computation.1 | async-start | bytes 3932160 | tf_op jit(solution)/shard_map/all_to_all | solution.py:373
  95.7 3.3 %collective-permute-start.11 = (bf16[128,2560]{1,0:T(8,128)(2,1)}, bf16[128,2560]{1,0:T(8,128)(2,1)S(1)}, u32[]{:S(2)}, u32[]{:S(2)}) collective-permute-start(bf16[128,2560]{1,0:T(8,128)(2,1)} %collective-permute-done.2.refs_2_), channel_id=1, source_target_pairs={{0,1},{1,0},{2,3},{3,2},{4,5},{5,4},{6,7},{7,6},{8,9},{9,8},{10,11... | collective-permute-start | bytes 1966088 | tf_op jit(solution)/shard_map/ppermute | solution.py:29
  99.1 11.7 %collective-permute-done.4.refs_0_.refs_6_ = bf16[128,2560]{1,0:T(8,128)(2,1)S(1)} collective-permute-done((bf16[128,2560]{1,0:T(8,128)(2,1)}, bf16[128,2560]{1,0:T(8,128)(2,1)S(1)}, u32[]{:S(2)}, u32[]{:S(2)}) %collective-permute-start.4) | collective-permute-done | bytes 655392 | tf_op jit(solution)/shard_map/ppermute | solution.py:350
  110.8 4.0 %collective-permute-start.5 = (bf16[128,2560]{1,0:T(8,128)(2,1)S(1)}, bf16[128,2560]{1,0:T(8,128)(2,1)S(1)}, u32[]{:S(2)}, u32[]{:S(2)}) collective-permute-start(bf16[128,2560]{1,0:T(8,128)(2,1)S(1)} %collective-permute-done.4.refs_0_.refs_6_), channel_id=1, source_target_pairs={{0,1},{1,0},{2,3},{3,2},{4,5},{5,4},{6,7},{7,6},{8,9},{9,8},{10,11... | collective-permute-start | bytes 1966088 | tf_op jit(solution)/shard_map/ppermute | solution.py:29
  116.5 4.8 %weight.2 = bf16[2560,384]{1,0:T(8,128)(2,1)S(1)} custom-call(s32[3]{0:T(128)S(1)} %pad_add_fusion.here_ref, bf16[128,5120]{1,0:T(8,128)(2,1)S(1)} %copy-done, bf16[128,5120]{1,0:T(8,128)(2,1)S(1)} %collective-permute-done.6.refs_1_, bf16[128,2560]{1,0:T(8,128)(2,1)} %collective-permute-done.2.refs_2_, ...), custom_call_target="tpu_custom_call" | custom-call | flops 2013265920 | bytes 7995392 | tf_op jit(solution)/shard_map/weight/pallas_call | solution.py:318
  126.0 6.7 %all-to-all-start = ((bf16[16,160,384]{2,1,0:T(8,128)(2,1)}), bf16[16,160,384]{2,1,0:T(8,128)(2,1)}, u32[]{:S(2)}, u32[]{:S(2)}) async-start(bf16[16,160,384]{2,1,0:T(8,128)(2,1)} %bitcast.5), calls=%async_computation | async-start | bytes 3932160 | tf_op jit(solution)/shard_map/all_to_all | solution.py:373
  132.7 5.9 %project.3.refs_7_.refs_3_ = f32[1024,384]{1,0:T(8,128)S(1)} custom-call(s32[3]{0:T(128)S(1)} %pad_add_fusion.here_ref, bf16[128,5120]{1,0:T(8,128)(2,1)S(1)} %copy-done, bf16[128,5120]{1,0:T(8,128)(2,1)S(1)} %collective-permute-done.6.refs_1_, bf16[128,2560]{1,0:T(8,128)(2,1)} %collective-permute-done.refs_2_, ...), custom_call_target="tpu_custom_call" | custom-call | flops 2013265920 | bytes 10354688 | tf_op jit(solution)/shard_map/project/pallas_call | solution.py:292
  138.6 4.8 %project.4.refs_4_ = bf16[1024,384]{1,0:T(8,128)(2,1)S(1)} custom-call(s32[3]{0:T(128)S(1)} %pad_add_fusion.here_ref, bf16[128,5120]{1,0:T(8,128)(2,1)S(1)} %copy-done, bf16[128,5120]{1,0:T(8,128)(2,1)S(1)} %collective-permute-done.6.refs_1_, bf16[128,2560]{1,0:T(8,128)(2,1)} %collective-permute-done.2.refs_2_, bf16[128,2560]{1,0:T(8,128)(2,1)S(1)} %copy-done.8, ...), custom_call_target="tpu_custom_call" | custom-call | flops 1509949440 | bytes 8257536 | tf_op jit(solution)/shard_map/project/pallas_call | solution.py:292
  143.5 3.3 %project.5.g_ref = bf16[1024,384]{1,0:T(8,128)(2,1)S(1)} custom-call(s32[3]{0:T(128)S(1)} %pad_add_fusion.here_ref, bf16[128,2560]{1,0:T(8,128)(2,1)S(1)} %copy-done.6, bf16[128,2560]{1,0:T(8,128)(2,1)S(1)} %copy-done.12, bf16[384,5120]{1,0:T(8,128)(2,1)} %refs_2_.1, f32[1024,384]{1,0:T(8,128)S(1)} %project.3.refs_7_.refs_3_, ...), custom_call_target="tpu_custom_call", output_to_operand_aliasing={{}: (5, {})} | custom-call | flops 503316480 | bytes 4063232 | tf_op jit(solution)/shard_map/project/pallas_call | solution.py:292
  146.9 8.9 %backward.1 = (bf16[1024,384]{1,0:T(8,128)(2,1)}, bf16[1024,384]{1,0:T(8,128)(2,1)}, bf16[1024,384]{1,0:T(8,128)(2,1)}, bf16[3,512,384]{2,1,0:T(8,128)(2,1)S(1)}) custom-call(s32[3]{0:T(128)S(1)} %pad_add_fusion.here_ref, s32[32,8]{1,0:T(8,128)S(1)} %copy.16.ids_ref, bf16[1024,384]{1,0:T(8,128)(2,1)S(1)} %copy-done.14, bf16[384,1024]{1,0:T(8,128)(2,1)S(1)} %copy-done.20, ...), custom_call_target="tpu_custom_call" | custom-call | flops 1610612736 | bytes 10616832 | tf_op jit(solution)/shard_map/backward/pallas_call | solution.py:192
  155.7 5.0 %collective-permute-start.13 = (bf16[3,512,384]{2,1,0:T(8,128)(2,1)S(1)}, bf16[3,512,384]{2,1,0:T(8,128)(2,1)S(1)}, u32[]{:S(2)}, u32[]{:S(2)}) collective-permute-start(bf16[3,512,384]{2,1,0:T(8,128)(2,1)S(1)} %get-tuple-element.25), channel_id=1, source_target_pairs={{0,128},{128,0},{1,129},{129,1},{2,130},{130,2},{3,131},{131,3},{4... | collective-permute-start | bytes 3538952 | tf_op jit(solution)/shard_map/ppermute | solution.py:29
  162.8 1.8 convert_reduce_fusion.1
  164.6 5.0 %collective-permute-start.14 = (bf16[160,384]{1,0:T(8,128)(2,1)S(1)}, bf16[160,384]{1,0:T(8,128)(2,1)S(1)}, u32[]{:S(2)}, u32[]{:S(2)}) collective-permute-start(bf16[160,384]{1,0:T(8,128)(2,1)S(1)} %select_convert_fusion), channel_id=1, source_target_pairs={{0,128},{128,0},{1,129},{129,1},{2,130},{130,2},{3,131},{131,3},{4... | collective-permute-start | bytes 368648 | tf_op jit(solution)/shard_map/ppermute | solution.py:29
  169.7 45.3 %collective-permute-done.13.refs_3_ = bf16[3,512,384]{2,1,0:T(8,128)(2,1)S(1)} collective-permute-done((bf16[3,512,384]{2,1,0:T(8,128)(2,1)S(1)}, bf16[3,512,384]{2,1,0:T(8,128)(2,1)S(1)}, u32[]{:S(2)}, u32[]{:S(2)}) %collective-permute-start.13) | collective-permute-done | bytes 1179680 | tf_op jit(solution)/shard_map/ppermute | solution.py:29
  (74 shorter events, 22.8 us)
Async XLA Ops:
  0.6 65.8 %copy-start.23 = (s32[32,8]{0,1:T(8,128)S(1)}, s32[32,8]{0,1:T(8,128)}, u32[]{:S(2)}) copy-start(s32[32,8]{0,1:T(8,128)} %param.12) | copy-start | bytes 3076
  1.8 77.6 %copy-start = (bf16[128,5120]{1,0:T(8,128)(2,1)S(1)}, bf16[128,5120]{1,0:T(8,128)(2,1)}, u32[]{:S(2)}) copy-start(bf16[128,5120]{1,0:T(8,128)(2,1)} %refs_0_.7) | copy-start | bytes 3932164
  1.8 18.9 %collective-permute-start = (bf16[128,2560]{1,0:T(8,128)(2,1)S(1)}, bf16[128,2560]{1,0:T(8,128)(2,1)}, u32[]{:S(2)}, u32[]{:S(2)}) collective-permute-start(bf16[128,2560]{1,0:T(8,128)(2,1)S(1)} %slice.6), channel_id=1, source_target_pairs={{0,2},{2,4},{4,6},{6,0},{1,3},{3,5},{5,7},{7,1},{8,10},{10,12},{12... | collective-permute-start | bytes 1966088 | tf_op jit(solution)/shard_map/ppermute | solution.py:350
  20.7 16.2 %collective-permute-start.1 = (bf16[128,2560]{1,0:T(8,128)(2,1)}, bf16[128,2560]{1,0:T(8,128)(2,1)}, u32[]{:S(2)}, u32[]{:S(2)}) collective-permute-start(bf16[128,2560]{1,0:T(8,128)(2,1)} %collective-permute-done.refs_2_), channel_id=1, source_target_pairs={{0,2},{2,4},{4,6},{6,0},{1,3},{3,5},{5,7},{7,1},{8,10},{10,12},{12... | collective-permute-start | bytes 1966088 | tf_op jit(solution)/shard_map/ppermute | solution.py:350
  20.7 58.7 %collective-permute-start.6 = (bf16[128,5120]{1,0:T(8,128)(2,1)}, bf16[128,5120]{1,0:T(8,128)(2,1)S(1)}, u32[]{:S(2)}, u32[]{:S(2)}) collective-permute-start(bf16[128,5120]{1,0:T(8,128)(2,1)} %refs_0_.7), channel_id=1, source_target_pairs={{0,1},{1,0},{2,3},{3,2},{4,5},{5,4},{6,7},{7,6},{8,9},{9,8},{10,11... | collective-permute-start | bytes 3932168 | tf_op jit(solution)/shard_map/ppermute | solution.py:29
  36.9 15.4 %collective-permute-start.9 = (bf16[128,2560]{1,0:T(8,128)(2,1)}, bf16[128,2560]{1,0:T(8,128)(2,1)}, u32[]{:S(2)}, u32[]{:S(2)}) collective-permute-start(bf16[128,2560]{1,0:T(8,128)(2,1)} %collective-permute-done.1.refs_4_), channel_id=1, source_target_pairs={{0,2},{2,4},{4,6},{6,0},{1,3},{3,5},{5,7},{7,1},{8,10},{10,12},{12... | collective-permute-start | bytes 1966088 | tf_op jit(solution)/shard_map/ppermute | solution.py:350
  38.1 28.3 %collective-permute-start.2 = (bf16[128,2560]{1,0:T(8,128)(2,1)S(1)}, bf16[128,2560]{1,0:T(8,128)(2,1)}, u32[]{:S(2)}, u32[]{:S(2)}) collective-permute-start(bf16[128,2560]{1,0:T(8,128)(2,1)S(1)} %slice.7), channel_id=1, source_target_pairs={{0,2},{2,4},{4,6},{6,0},{1,3},{3,5},{5,7},{7,1},{8,10},{10,12},{12... | collective-permute-start | bytes 1966088 | tf_op jit(solution)/shard_map/ppermute | solution.py:350
  38.1 41.3 %collective-permute-start.7 = (bf16[128,2560]{1,0:T(8,128)(2,1)}, bf16[128,2560]{1,0:T(8,128)(2,1)}, u32[]{:S(2)}, u32[]{:S(2)}) collective-permute-start(bf16[128,2560]{1,0:T(8,128)(2,1)} %collective-permute-done.refs_2_), channel_id=1, source_target_pairs={{0,1},{1,0},{2,3},{3,2},{4,5},{5,4},{6,7},{7,6},{8,9},{9,8},{10,11... | collective-permute-start | bytes 1966088 | tf_op jit(solution)/shard_map/ppermute | solution.py:29
  41.2 38.2 %collective-permute-start.8 = (bf16[128,2560]{1,0:T(8,128)(2,1)}, bf16[128,2560]{1,0:T(8,128)(2,1)}, u32[]{:S(2)}, u32[]{:S(2)}) collective-permute-start(bf16[128,2560]{1,0:T(8,128)(2,1)} %collective-permute-done.1.refs_4_), channel_id=1, source_target_pairs={{0,1},{1,0},{2,3},{3,2},{4,5},{5,4},{6,7},{7,6},{8,9},{9,8},{10,11... | collective-permute-start | bytes 1966088 | tf_op jit(solution)/shard_map/ppermute | solution.py:29
  52.3 27.1 %collective-permute-start.10 = (bf16[128,2560]{1,0:T(8,128)(2,1)}, bf16[128,2560]{1,0:T(8,128)(2,1)}, u32[]{:S(2)}, u32[]{:S(2)}) collective-permute-start(bf16[128,2560]{1,0:T(8,128)(2,1)} %collective-permute-done.9.refs_6_), channel_id=1, source_target_pairs={{0,1},{1,0},{2,3},{3,2},{4,5},{5,4},{6,7},{7,6},{8,9},{9,8},{10,11... | collective-permute-start | bytes 1966088 | tf_op jit(solution)/shard_map/ppermute | solution.py:29
  66.4 29.2 %collective-permute-start.3 = (bf16[128,2560]{1,0:T(8,128)(2,1)}, bf16[128,2560]{1,0:T(8,128)(2,1)}, u32[]{:S(2)}, u32[]{:S(2)}) collective-permute-start(bf16[128,2560]{1,0:T(8,128)(2,1)} %collective-permute-done.2.refs_2_), channel_id=1, source_target_pairs={{0,2},{2,4},{4,6},{6,0},{1,3},{3,5},{5,7},{7,1},{8,10},{10,12},{12... | collective-permute-start | bytes 1966088 | tf_op jit(solution)/shard_map/ppermute | solution.py:350
  86.0 40.0 %all-to-all-start.1 = ((bf16[16,160,384]{2,1,0:T(8,128)(2,1)}), bf16[16,160,384]{2,1,0:T(8,128)(2,1)}, u32[]{:S(2)}, u32[]{:S(2)}) async-start(bf16[16,160,384]{2,1,0:T(8,128)(2,1)} %bitcast.6), calls=%async_computation.1 | async-start | bytes 3932160 | tf_op jit(solution)/shard_map/all_to_all | solution.py:373
  95.6 15.2 %collective-permute-start.4 = (bf16[128,2560]{1,0:T(8,128)(2,1)}, bf16[128,2560]{1,0:T(8,128)(2,1)S(1)}, u32[]{:S(2)}, u32[]{:S(2)}) collective-permute-start(bf16[128,2560]{1,0:T(8,128)(2,1)} %collective-permute-done.3.refs_4_), channel_id=1, source_target_pairs={{0,2},{2,4},{4,6},{6,0},{1,3},{3,5},{5,7},{7,1},{8,10},{10,12},{12... | collective-permute-start | bytes 1966088 | tf_op jit(solution)/shard_map/ppermute | solution.py:350
  95.7 19.1 %collective-permute-start.11 = (bf16[128,2560]{1,0:T(8,128)(2,1)}, bf16[128,2560]{1,0:T(8,128)(2,1)S(1)}, u32[]{:S(2)}, u32[]{:S(2)}) collective-permute-start(bf16[128,2560]{1,0:T(8,128)(2,1)} %collective-permute-done.2.refs_2_), channel_id=1, source_target_pairs={{0,1},{1,0},{2,3},{3,2},{4,5},{5,4},{6,7},{7,6},{8,9},{9,8},{10,11... | collective-permute-start | bytes 1966088 | tf_op jit(solution)/shard_map/ppermute | solution.py:29
  99.0 15.8 %collective-permute-start.12 = (bf16[128,2560]{1,0:T(8,128)(2,1)}, bf16[128,2560]{1,0:T(8,128)(2,1)S(1)}, u32[]{:S(2)}, u32[]{:S(2)}) collective-permute-start(bf16[128,2560]{1,0:T(8,128)(2,1)} %collective-permute-done.3.refs_4_), channel_id=1, source_target_pairs={{0,1},{1,0},{2,3},{3,2},{4,5},{5,4},{6,7},{7,6},{8,9},{9,8},{10,11... | collective-permute-start | bytes 1966088 | tf_op jit(solution)/shard_map/ppermute | solution.py:29
  110.8 5.7 %collective-permute-start.5 = (bf16[128,2560]{1,0:T(8,128)(2,1)S(1)}, bf16[128,2560]{1,0:T(8,128)(2,1)S(1)}, u32[]{:S(2)}, u32[]{:S(2)}) collective-permute-start(bf16[128,2560]{1,0:T(8,128)(2,1)S(1)} %collective-permute-done.4.refs_0_.refs_6_), channel_id=1, source_target_pairs={{0,1},{1,0},{2,3},{3,2},{4,5},{5,4},{6,7},{7,6},{8,9},{9,8},{10,11... | collective-permute-start | bytes 1966088 | tf_op jit(solution)/shard_map/ppermute | solution.py:29
  126.0 36.7 %all-to-all-start = ((bf16[16,160,384]{2,1,0:T(8,128)(2,1)}), bf16[16,160,384]{2,1,0:T(8,128)(2,1)}, u32[]{:S(2)}, u32[]{:S(2)}) async-start(bf16[16,160,384]{2,1,0:T(8,128)(2,1)} %bitcast.5), calls=%async_computation | async-start | bytes 3932160 | tf_op jit(solution)/shard_map/all_to_all | solution.py:373
  132.7 5.9 %copy-start.8 = (bf16[128,2560]{1,0:T(8,128)(2,1)S(1)}, bf16[128,2560]{1,0:T(8,128)(2,1)}, u32[]{:S(2)}) copy-start(bf16[128,2560]{1,0:T(8,128)(2,1)} %copy-done.7) | copy-start | bytes 1966084
  132.7 5.9 %copy-start.10 = (bf16[128,2560]{1,0:T(8,128)(2,1)S(1)}, bf16[128,2560]{1,0:T(8,128)(2,1)}, u32[]{:S(2)}) copy-start(bf16[128,2560]{1,0:T(8,128)(2,1)} %copy-done.9) | copy-start | bytes 1966084
  138.6 4.8 %copy-start.6 = (bf16[128,2560]{1,0:T(8,128)(2,1)S(1)}, bf16[128,2560]{1,0:T(8,128)(2,1)}, u32[]{:S(2)}) copy-start(bf16[128,2560]{1,0:T(8,128)(2,1)} %copy-done.5) | copy-start | bytes 1966084
  138.6 4.8 %copy-start.12 = (bf16[128,2560]{1,0:T(8,128)(2,1)S(1)}, bf16[128,2560]{1,0:T(8,128)(2,1)}, u32[]{:S(2)}) copy-start(bf16[128,2560]{1,0:T(8,128)(2,1)} %copy-done.11) | copy-start | bytes 1966084
  155.7 59.2 %collective-permute-start.13 = (bf16[3,512,384]{2,1,0:T(8,128)(2,1)S(1)}, bf16[3,512,384]{2,1,0:T(8,128)(2,1)S(1)}, u32[]{:S(2)}, u32[]{:S(2)}) collective-permute-start(bf16[3,512,384]{2,1,0:T(8,128)(2,1)S(1)} %get-tuple-element.25), channel_id=1, source_target_pairs={{0,128},{128,0},{1,129},{129,1},{2,130},{130,2},{3,131},{131,3},{4... | collective-permute-start | bytes 3538952 | tf_op jit(solution)/shard_map/ppermute | solution.py:29
  162.6 52.4 %copy-start.21 = (s32[32]{0:T(128)S(1)}, s32[32]{0:T(128)}, u32[]{:S(2)}) copy-start(s32[32]{0:T(128)} %counts_ref.1) | copy-start | bytes 388
  164.6 52.9 %collective-permute-start.14 = (bf16[160,384]{1,0:T(8,128)(2,1)S(1)}, bf16[160,384]{1,0:T(8,128)(2,1)S(1)}, u32[]{:S(2)}, u32[]{:S(2)}) collective-permute-start(bf16[160,384]{1,0:T(8,128)(2,1)S(1)} %select_convert_fusion), channel_id=1, source_target_pairs={{0,128},{128,0},{1,129},{129,1},{2,130},{130,2},{3,131},{131,3},{4... | collective-permute-start | bytes 368648 | tf_op jit(solution)/shard_map/ppermute | solution.py:29
  (17 other events, 29.7 us)

commit v2 on v1

--- a/solution.py
+++ b/solution.py
@@ -78,9 +78,9 @@
 
 
 def backward_kernel(
-    here_ref, ids_ref, q_ref, kt_ref, v_ref, g_ref, o_ref, p_ref,
-    dq_ref, dk_ref, dv_ref, tail_ref, ka, va,
+    here_ref, ids_ref, q_ref, kt_ref, v_ref, g_ref, o_ref, p_ref, *rest
 ):
+    dq_ref, dk_ref, dv_ref, tail_ref, ka, va = rest[-6:]
     row = here_ref[0]
     front = dq_ref.shape[0] - tail_ref.shape[1]
     ka[...] = jnp.zeros_like(ka)
@@ -104,7 +104,7 @@
         tail_ref[i] = ref[front:, :]
 
 
-def settle_kernel(here_ref, counts_ref, *refs):
+def settle_kernel(column, here_ref, counts_ref, *refs):
     arrived_ref, outs, sems = refs[3], refs[4:7], refs[7]
     moving = counts_ref[here_ref[0]]
     front = outs[0].shape[0] - arrived_ref.shape[1]
@@ -112,7 +112,7 @@
     def copy(i, b):
         return pltpu.make_async_copy(
             arrived_ref.at[i, pl.ds(b * BLOCK, BLOCK), :],
-            outs[i].at[pl.ds(front + b * BLOCK, BLOCK), :],
+            outs[i].at[pl.ds(front + b * BLOCK, BLOCK), pl.ds(column, arrived_ref.shape[2])],
             sems.at[i, b],
         )
 
@@ -181,34 +181,38 @@
     )(here, ids, q, k, v)
 
 
-def backward(here, ids, q, kt, v, g, o, p):
+def backward(here, ids, first, heads, q, kt, v, g, o, p, before):
     rows, inner = q.shape
-    heads, blocks = inner // HEAD_SIZE, rows // BLOCK
+    blocks = rows // BLOCK
     keys = WINDOW * BLOCK
     moving = MOVABLE * BLOCK
-    hs = pl.BlockSpec((rows, HEAD_SIZE), lambda h, *_: (0, h))
-    ps = pl.BlockSpec((1, blocks, keys, BLOCK), lambda h, *_: (h, 0, 0, 0))
-    ts = pl.BlockSpec((HEAD_SIZE, rows), lambda h, *_: (h, 0))
+    hs = pl.BlockSpec((rows, HEAD_SIZE), lambda h, *_: (0, first + h))
+    ps = pl.BlockSpec((1, blocks, keys, BLOCK), lambda h, *_: (first + h, 0, 0, 0))
+    ts = pl.BlockSpec((HEAD_SIZE, rows), lambda h, *_: (first + h, 0))
     return pl.pallas_call(
         backward_kernel,
         grid_spec=prefetched(
             2,
             (heads,),
-            [hs, ts, hs, hs, hs, ps],
+            [hs, ts, hs, hs, hs, ps] + [ANY] * len(before),
             [hs] * 3 + [pl.BlockSpec((3, moving, HEAD_SIZE), lambda h, *_: (0, 0, h))],
             [pltpu.VMEM((rows, HEAD_SIZE), jnp.float32)] * 2,
         ),
         out_shape=[jax.ShapeDtypeStruct((rows, inner), jnp.bfloat16)] * 3
-        + [jax.ShapeDtypeStruct((3, moving, inner), jnp.bfloat16)],
+        + [jax.ShapeDtypeStruct((3, moving, heads * HEAD_SIZE), jnp.bfloat16)],
+        input_output_aliases={8 + i: i for i in range(len(before))},
         compiler_params=room(20),
-        cost_estimate=cost(8 * rows * keys * inner, 19 * rows * inner + 2 * heads * rows * keys),
+        cost_estimate=cost(
+            8 * rows * keys * heads * HEAD_SIZE,
+            19 * rows * heads * HEAD_SIZE + 2 * heads * rows * keys,
+        ),
         name="backward",
-    )(here, ids, q, kt, v, g, o, p)
-
-
-def settle(here, counts, local, arrived):
+    )(here, ids, q, kt, v, g, o, p, *before)
+
+
+def settle(here, counts, first, local, arrived):
     return pl.pallas_call(
-        settle_kernel,
+        functools.partial(settle_kernel, first * HEAD_SIZE),
         grid_spec=prefetched(
             2,
             (1,),
@@ -378,11 +382,16 @@
     got = swapped(sent, "z_hi")
     weight_gradient = kept + got.astype(jnp.float32)
 
-    *local, tail = backward(
-        here, segments, queries, keys_turned, values, gradient, head_output, chances
-    )
-    arrived = swapped(tail, "z_hi")
-    local = settle(here, counts, local, arrived)
+    local, arrived = [], []
+    shares = ((0, 2), (2, 1))
+    for first, heads in shares:
+        *local, tail = backward(
+            here, segments, first, heads,
+            queries, keys_turned, values, gradient, head_output, chances, local,
+        )
+        arrived.append(swapped(tail, "z_hi"))
+    for i, (first, _) in enumerate(shares):
+        local = settle(here, counts, first, local, arrived[i])
     return (*local, weight_gradient)
 
 

time: 219 us -> 217 us (level)
  waiting for transfers between devices: 108 us -> 102 us
  Pallas kernels: 40.6 us -> 43.3 us
    ppermute x9 -> x10, waiting for transfers between devices: 48 us -> 42.7 us  [swapped(): return lax.ppermute(x, axis, [(i, (i + n // 2) % n) for i in range(n)])]
    pallas_call x1 -> x2, Pallas kernels: 8.87 us -> 10.3 us  [backward(): pl.pallas_call(backward_kernel, grid_spec=prefetched(2, (heads,), [hs, ts...]
    ppermute x9 -> x10, starting transfers between devices: 30.1 us -> 30.3 us  [swapped(): return lax.ppermute(x, axis, [(i, (i + n // 2) % n) for i in range(n)])]
    unnamed x49 -> x51, local copies, waits for them, and re-layouts: 12.9 us -> 13 us
  transfers between devices with their start and end apart: 17 -> 18, of which waited for: 9 -> 9; matrix products, arithmetic and copies ran while one was open for 2% -> 3% of each run, Pallas kernels for 19% -> 20%
where the time goes in v2:
time: 217 us; the launch traced here: 216 us
  waiting for transfers between devices  102 us (47%)
  starting transfers between devices  49.1 us (23%)
  Pallas kernels  43.3 us (20%)
  local copies, waits for them, and re-layouts  16.1 us (7%)
  other arithmetic  4.52 us (2%)
    ppermute x6, waiting for transfers between devices, turn(): y = lax.ppermute(x, 'z_lo', ring)  59.3 us
    ppermute x10, waiting for transfers between devices, swapped(): return lax.ppermute(x, axis, [(i, (i + n // 2) % n) for i in range(n)])  42.7 us
    ppermute x10, starting transfers between devices, swapped(): return lax.ppermute(x, axis, [(i, (i + n // 2) % n) for i in range(n)])  30.3 us
    all_to_all x2, starting transfers between devices, steps(): tiles = lax.all_to_all(tiles, ('y', 'x'), 0, 0, tiled=True)  16.2 us
    pallas_call x3, Pallas kernels, project(): pl.pallas_call(functools.partial(project_kernel, turns, final), grid_spec...  13.9 us
    unnamed x51, local copies, waits for them, and re-layouts  13 us
    pallas_call x2, Pallas kernels, backward(): pl.pallas_call(backward_kernel, grid_spec=prefetched(2, (heads,), [hs, ts...  10.3 us
    pallas_call x2, Pallas kernels, weight(): pl.pallas_call(weight_kernel, grid_spec=prefetched(1, (depth // width,),...  10.1 us
  transfers between devices with their start and end apart: 18, of which 9 were waited for; matrix products, arithmetic and copies ran while one was open for 3% of the time, Pallas kernels for 20%

profile of v2, /device:TPU:1, one launch (start us, length us, event | category | flops | bytes accessed | tf_op | source)
XLA Modules:
  0.0 216.0 jit_solution(9700541201370945241)
XLA Ops:
  1.9 2.5 %collective-permute-start = (bf16[128,2560]{1,0:T(8,128)(2,1)S(1)}, bf16[128,2560]{1,0:T(8,128)(2,1)}, u32[]{:S(2)}, u32[]{:S(2)}) collective-permute-start(bf16[128,2560]{1,0:T(8,128)(2,1)S(1)} %slice.6), channel_id=1, source_target_pairs={{0,2},{2,4},{4,6},{6,0},{1,3},{3,5},{5,7},{7,1},{8,10},{10,12},{12... | collective-permute-start | bytes 1966088 | tf_op jit(solution)/shard_map/ppermute | solution.py:354
  4.4 16.3 %collective-permute-done.refs_2_ = bf16[128,2560]{1,0:T(8,128)(2,1)} collective-permute-done((bf16[128,2560]{1,0:T(8,128)(2,1)S(1)}, bf16[128,2560]{1,0:T(8,128)(2,1)}, u32[]{:S(2)}, u32[]{:S(2)}) %collective-permute-start) | collective-permute-done | bytes 655392 | tf_op jit(solution)/shard_map/ppermute | solution.py:354
  22.9 14.1 %collective-permute-done.1.refs_4_ = bf16[128,2560]{1,0:T(8,128)(2,1)} collective-permute-done((bf16[128,2560]{1,0:T(8,128)(2,1)}, bf16[128,2560]{1,0:T(8,128)(2,1)}, u32[]{:S(2)}, u32[]{:S(2)}) %collective-permute-start.1) | collective-permute-done | bytes 655392 | tf_op jit(solution)/shard_map/ppermute | solution.py:354
  39.0 3.0 %collective-permute-start.7 = (bf16[128,2560]{1,0:T(8,128)(2,1)}, bf16[128,2560]{1,0:T(8,128)(2,1)}, u32[]{:S(2)}, u32[]{:S(2)}) collective-permute-start(bf16[128,2560]{1,0:T(8,128)(2,1)} %collective-permute-done.refs_2_), channel_id=1, source_target_pairs={{0,1},{1,0},{2,3},{3,2},{4,5},{5,4},{6,7},{7,6},{8,9},{9,8},{10,11... | collective-permute-start | bytes 1966088 | tf_op jit(solution)/shard_map/ppermute | solution.py:29
  42.0 10.4 %collective-permute-done.9.refs_6_ = bf16[128,2560]{1,0:T(8,128)(2,1)} collective-permute-done((bf16[128,2560]{1,0:T(8,128)(2,1)}, bf16[128,2560]{1,0:T(8,128)(2,1)}, u32[]{:S(2)}, u32[]{:S(2)}) %collective-permute-start.9) | collective-permute-done | bytes 655392 | tf_op jit(solution)/shard_map/ppermute | solution.py:354
  52.4 7.3 %collective-permute-start.10 = (bf16[128,2560]{1,0:T(8,128)(2,1)}, bf16[128,2560]{1,0:T(8,128)(2,1)}, u32[]{:S(2)}, u32[]{:S(2)}) collective-permute-start(bf16[128,2560]{1,0:T(8,128)(2,1)} %collective-permute-done.9.refs_6_), channel_id=1, source_target_pairs={{0,1},{1,0},{2,3},{3,2},{4,5},{5,4},{6,7},{7,6},{8,9},{9,8},{10,11... | collective-permute-start | bytes 1966088 | tf_op jit(solution)/shard_map/ppermute | solution.py:29
  59.7 6.7 %collective-permute-done.2.refs_2_ = bf16[128,2560]{1,0:T(8,128)(2,1)} collective-permute-done((bf16[128,2560]{1,0:T(8,128)(2,1)}, bf16[128,2560]{1,0:T(8,128)(2,1)}, u32[]{:S(2)}, u32[]{:S(2)}) %collective-permute-start.2) | collective-permute-done | bytes 655392 | tf_op jit(solution)/shard_map/ppermute | solution.py:354
  68.9 6.1 %forward.1 = (bf16[3,8,512,128]{3,2,1,0:T(8,128)(2,1)S(1)}, bf16[1024,384]{1,0:T(8,128)(2,1)S(1)}, bf16[1024,384]{1,0:T(8,128)(2,1)S(1)}, bf16[384,1024]{1,0:T(8,128)(2,1)S(1)}) custom-call(s32[3]{0:T(128)S(1)} %pad_add_fusion.here_ref, s32[32,8]{1,0:T(8,128)S(1)} %copy.23.ids_ref, bf16[1024,384]{1,0:T(8,128)(2,1)S(1)} %copy-done.5, ...), custom_call_target="tpu_custom_call" | custom-call | flops 805306368 | bytes 7864320 | tf_op jit(solution)/shard_map/forward/pallas_call | solution.py:159
  78.4 5.2 %weight.3 = bf16[2560,384]{1,0:T(8,128)(2,1)S(1)} custom-call(s32[3]{0:T(128)S(1)} %pad_add_fusion.here_ref, bf16[128,5120]{1,0:T(8,128)(2,1)S(1)} %copy-done, bf16[128,5120]{1,0:T(8,128)(2,1)S(1)} %collective-permute-done.6.refs_1_, bf16[128,2560]{1,0:T(8,128)(2,1)} %collective-permute-done.refs_2_, bf16[128,2560]{1,0:T(8,128)(2,1)} %collective-permute-done.7.refs_3_, ...), custom_call_target="tpu_custom_call" | custom-call | flops 2013265920 | bytes 7995392 | tf_op jit(solution)/shard_map/weight/pallas_call | solution.py:322
  85.0 9.5 %all-to-all-start.1 = ((bf16[16,160,384]{2,1,0:T(8,128)(2,1)}), bf16[16,160,384]{2,1,0:T(8,128)(2,1)}, u32[]{:S(2)}, u32[]{:S(2)}) async-start(bf16[16,160,384]{2,1,0:T(8,128)(2,1)} %bitcast.6), calls=%async_computation.1 | async-start | bytes 3932160 | tf_op jit(solution)/shard_map/all_to_all | solution.py:377
  94.7 3.3 %collective-permute-start.11 = (bf16[128,2560]{1,0:T(8,128)(2,1)}, bf16[128,2560]{1,0:T(8,128)(2,1)S(1)}, u32[]{:S(2)}, u32[]{:S(2)}) collective-permute-start(bf16[128,2560]{1,0:T(8,128)(2,1)} %collective-permute-done.2.refs_2_), channel_id=1, source_target_pairs={{0,1},{1,0},{2,3},{3,2},{4,5},{5,4},{6,7},{7,6},{8,9},{9,8},{10,11... | collective-permute-start | bytes 1966088 | tf_op jit(solution)/shard_map/ppermute | solution.py:29
  98.1 11.7 %collective-permute-done.4.refs_0_.refs_6_ = bf16[128,2560]{1,0:T(8,128)(2,1)S(1)} collective-permute-done((bf16[128,2560]{1,0:T(8,128)(2,1)}, bf16[128,2560]{1,0:T(8,128)(2,1)S(1)}, u32[]{:S(2)}, u32[]{:S(2)}) %collective-permute-start.4) | collective-permute-done | bytes 655392 | tf_op jit(solution)/shard_map/ppermute | solution.py:354
  109.8 4.0 %collective-permute-start.5 = (bf16[128,2560]{1,0:T(8,128)(2,1)S(1)}, bf16[128,2560]{1,0:T(8,128)(2,1)S(1)}, u32[]{:S(2)}, u32[]{:S(2)}) collective-permute-start(bf16[128,2560]{1,0:T(8,128)(2,1)S(1)} %collective-permute-done.4.refs_0_.refs_6_), channel_id=1, source_target_pairs={{0,1},{1,0},{2,3},{3,2},{4,5},{5,4},{6,7},{7,6},{8,9},{9,8},{10,11... | collective-permute-start | bytes 1966088 | tf_op jit(solution)/shard_map/ppermute | solution.py:29
  116.7 4.8 %weight.2 = bf16[2560,384]{1,0:T(8,128)(2,1)S(1)} custom-call(s32[3]{0:T(128)S(1)} %pad_add_fusion.here_ref, bf16[128,5120]{1,0:T(8,128)(2,1)S(1)} %copy-done, bf16[128,5120]{1,0:T(8,128)(2,1)S(1)} %collective-permute-done.6.refs_1_, bf16[128,2560]{1,0:T(8,128)(2,1)} %collective-permute-done.2.refs_2_, ...), custom_call_target="tpu_custom_call" | custom-call | flops 2013265920 | bytes 7995392 | tf_op jit(solution)/shard_map/weight/pallas_call | solution.py:322
  126.2 6.7 %all-to-all-start = ((bf16[16,160,384]{2,1,0:T(8,128)(2,1)}), bf16[16,160,384]{2,1,0:T(8,128)(2,1)}, u32[]{:S(2)}, u32[]{:S(2)}) async-start(bf16[16,160,384]{2,1,0:T(8,128)(2,1)} %bitcast.5), calls=%async_computation | async-start | bytes 3932160 | tf_op jit(solution)/shard_map/all_to_all | solution.py:377
  132.9 5.9 %project.3.refs_7_.refs_3_ = f32[1024,384]{1,0:T(8,128)S(1)} custom-call(s32[3]{0:T(128)S(1)} %pad_add_fusion.here_ref, bf16[128,5120]{1,0:T(8,128)(2,1)S(1)} %copy-done, bf16[128,5120]{1,0:T(8,128)(2,1)S(1)} %collective-permute-done.6.refs_1_, bf16[128,2560]{1,0:T(8,128)(2,1)} %collective-permute-done.refs_2_, ...), custom_call_target="tpu_custom_call" | custom-call | flops 2013265920 | bytes 10354688 | tf_op jit(solution)/shard_map/project/pallas_call | solution.py:296
  138.8 4.8 %project.4.refs_4_ = bf16[1024,384]{1,0:T(8,128)(2,1)S(1)} custom-call(s32[3]{0:T(128)S(1)} %pad_add_fusion.here_ref, bf16[128,5120]{1,0:T(8,128)(2,1)S(1)} %copy-done, bf16[128,5120]{1,0:T(8,128)(2,1)S(1)} %collective-permute-done.6.refs_1_, bf16[128,2560]{1,0:T(8,128)(2,1)} %collective-permute-done.2.refs_2_, bf16[128,2560]{1,0:T(8,128)(2,1)S(1)} %copy-done.17, ...), custom_call_target="tpu_custom_call" | custom-call | flops 1509949440 | bytes 8257536 | tf_op jit(solution)/shard_map/project/pallas_call | solution.py:296
  143.6 3.3 %project.5.g_ref = bf16[1024,384]{1,0:T(8,128)(2,1)S(1)} custom-call(s32[3]{0:T(128)S(1)} %pad_add_fusion.here_ref, bf16[128,2560]{1,0:T(8,128)(2,1)S(1)} %copy-done.15, bf16[128,2560]{1,0:T(8,128)(2,1)S(1)} %copy-done.21, bf16[384,5120]{1,0:T(8,128)(2,1)} %refs_2_.1, f32[1024,384]{1,0:T(8,128)S(1)} %project.3.refs_7_.refs_3_, ...), custom_call_target="tpu_custom_call", output_to_operand_aliasing={{}: (5, {})} | custom-call | flops 503316480 | bytes 4063232 | tf_op jit(solution)/shard_map/project/pallas_call | solution.py:296
  147.0 6.4 %backward.2 = (bf16[1024,384]{1,0:T(8,128)(2,1)}, bf16[1024,384]{1,0:T(8,128)(2,1)}, bf16[1024,384]{1,0:T(8,128)(2,1)}, bf16[3,512,256]{2,1,0:T(8,128)(2,1)S(1)}) custom-call(s32[3]{0:T(128)S(1)} %pad_add_fusion.here_ref, s32[32,8]{1,0:T(8,128)S(1)} %copy.23.ids_ref, bf16[1024,384]{1,0:T(8,128)(2,1)S(1)} %copy-done.5, bf16[384,1024]{1,0:T(8,128)(2,1)S(1)} %copy-done.11, ...), custom_call_target="tpu_custom_call" | custom-call | flops 1073741824 | bytes 7077888 | tf_op jit(solution)/shard_map/backward/pallas_call | solution.py:192
  153.4 4.9 %collective-permute-start.13 = (bf16[3,512,256]{2,1,0:T(8,128)(2,1)S(1)}, bf16[3,512,256]{2,1,0:T(8,128)(2,1)S(1)}, u32[]{:S(2)}, u32[]{:S(2)}) collective-permute-start(bf16[3,512,256]{2,1,0:T(8,128)(2,1)S(1)} %get-tuple-element.35), channel_id=1, source_target_pairs={{0,128},{128,0},{1,129},{129,1},{2,130},{130,2},{3,131},{131,3},{4... | collective-permute-start | bytes 2359304 | tf_op jit(solution)/shard_map/ppermute | solution.py:29
  158.4 3.8 %backward.3 = (bf16[1024,384]{1,0:T(8,128)(2,1)}, bf16[1024,384]{1,0:T(8,128)(2,1)}, bf16[1024,384]{1,0:T(8,128)(2,1)}, bf16[3,512,128]{2,1,0:T(8,128)(2,1)S(1)}) custom-call(s32[3]{0:T(128)S(1)} %pad_add_fusion.here_ref, s32[32,8]{1,0:T(8,128)S(1)} %copy.23.ids_ref, ...), custom_call_target="tpu_custom_call", output_to_operand_aliasing={{0}: (8, {}), {1}: (9, {}), {2}: (10, {})} | custom-call | flops 536870912 | bytes 3538944 | tf_op jit(solution)/shard_map/backward/pallas_call | solution.py:192
  166.4 5.0 %collective-permute-start.15 = (bf16[160,384]{1,0:T(8,128)(2,1)S(1)}, bf16[160,384]{1,0:T(8,128)(2,1)S(1)}, u32[]{:S(2)}, u32[]{:S(2)}) collective-permute-start(bf16[160,384]{1,0:T(8,128)(2,1)S(1)} %select_convert_fusion), channel_id=1, source_target_pairs={{0,128},{128,0},{1,129},{129,1},{2,130},{130,2},{3,131},{131,3},{4... | collective-permute-start | bytes 368648 | tf_op jit(solution)/shard_map/ppermute | solution.py:29
  171.4 22.9 %collective-permute-done.13.refs_3_ = bf16[3,512,256]{2,1,0:T(8,128)(2,1)S(1)} collective-permute-done((bf16[3,512,256]{2,1,0:T(8,128)(2,1)S(1)}, bf16[3,512,256]{2,1,0:T(8,128)(2,1)S(1)}, u32[]{:S(2)}, u32[]{:S(2)}) %collective-permute-start.13) | collective-permute-done | bytes 786464 | tf_op jit(solution)/shard_map/ppermute | solution.py:29
  195.8 16.8 %collective-permute-done.14.refs_3_ = bf16[3,512,128]{2,1,0:T(8,128)(2,1)S(1)} collective-permute-done((bf16[3,512,128]{2,1,0:T(8,128)(2,1)S(1)}, bf16[3,512,128]{2,1,0:T(8,128)(2,1)S(1)}, u32[]{:S(2)}, u32[]{:S(2)}) %collective-permute-start.14) | collective-permute-done | bytes 393248 | tf_op jit(solution)/shard_map/ppermute | solution.py:29
  (80 shorter events, 29.3 us)
Async XLA Ops:
  0.6 65.9 %copy-start.24 = (s32[32,8]{0,1:T(8,128)S(1)}, s32[32,8]{0,1:T(8,128)}, u32[]{:S(2)}) copy-start(s32[32,8]{0,1:T(8,128)} %param.12) | copy-start | bytes 3076
  0.6 66.0 %copy-start.5 = (bf16[1024,384]{1,0:T(8,128)(2,1)S(1)}, bf16[1024,384]{1,0:T(8,128)(2,1)}, u32[]{:S(2)}) copy-start(bf16[1024,384]{1,0:T(8,128)(2,1)} %q_ref.5) | copy-start | bytes 2359300
  1.9 76.5 %copy-start = (bf16[128,5120]{1,0:T(8,128)(2,1)S(1)}, bf16[128,5120]{1,0:T(8,128)(2,1)}, u32[]{:S(2)}) copy-start(bf16[128,5120]{1,0:T(8,128)(2,1)} %refs_0_.7) | copy-start | bytes 3932164
  1.9 18.9 %collective-permute-start = (bf16[128,2560]{1,0:T(8,128)(2,1)S(1)}, bf16[128,2560]{1,0:T(8,128)(2,1)}, u32[]{:S(2)}, u32[]{:S(2)}) collective-permute-start(bf16[128,2560]{1,0:T(8,128)(2,1)S(1)} %slice.6), channel_id=1, source_target_pairs={{0,2},{2,4},{4,6},{6,0},{1,3},{3,5},{5,7},{7,1},{8,10},{10,12},{12... | collective-permute-start | bytes 1966088 | tf_op jit(solution)/shard_map/ppermute | solution.py:354
  20.7 16.2 %collective-permute-start.1 = (bf16[128,2560]{1,0:T(8,128)(2,1)}, bf16[128,2560]{1,0:T(8,128)(2,1)}, u32[]{:S(2)}, u32[]{:S(2)}) collective-permute-start(bf16[128,2560]{1,0:T(8,128)(2,1)} %collective-permute-done.refs_2_), channel_id=1, source_target_pairs={{0,2},{2,4},{4,6},{6,0},{1,3},{3,5},{5,7},{7,1},{8,10},{10,12},{12... | collective-permute-start | bytes 1966088 | tf_op jit(solution)/shard_map/ppermute | solution.py:354
  20.8 57.6 %collective-permute-start.6 = (bf16[128,5120]{1,0:T(8,128)(2,1)}, bf16[128,5120]{1,0:T(8,128)(2,1)S(1)}, u32[]{:S(2)}, u32[]{:S(2)}) collective-permute-start(bf16[128,5120]{1,0:T(8,128)(2,1)} %refs_0_.7), channel_id=1, source_target_pairs={{0,1},{1,0},{2,3},{3,2},{4,5},{5,4},{6,7},{7,6},{8,9},{9,8},{10,11... | collective-permute-start | bytes 3932168 | tf_op jit(solution)/shard_map/ppermute | solution.py:29
  37.0 15.4 %collective-permute-start.9 = (bf16[128,2560]{1,0:T(8,128)(2,1)}, bf16[128,2560]{1,0:T(8,128)(2,1)}, u32[]{:S(2)}, u32[]{:S(2)}) collective-permute-start(bf16[128,2560]{1,0:T(8,128)(2,1)} %collective-permute-done.1.refs_4_), channel_id=1, source_target_pairs={{0,2},{2,4},{4,6},{6,0},{1,3},{3,5},{5,7},{7,1},{8,10},{10,12},{12... | collective-permute-start | bytes 1966088 | tf_op jit(solution)/shard_map/ppermute | solution.py:354
  39.0 27.5 %collective-permute-start.2 = (bf16[128,2560]{1,0:T(8,128)(2,1)}, bf16[128,2560]{1,0:T(8,128)(2,1)}, u32[]{:S(2)}, u32[]{:S(2)}) collective-permute-start(bf16[128,2560]{1,0:T(8,128)(2,1)} %slice.7), channel_id=1, source_target_pairs={{0,2},{2,4},{4,6},{6,0},{1,3},{3,5},{5,7},{7,1},{8,10},{10,12},{12... | collective-permute-start | bytes 1966088 | tf_op jit(solution)/shard_map/ppermute | solution.py:354
  39.0 39.4 %collective-permute-start.7 = (bf16[128,2560]{1,0:T(8,128)(2,1)}, bf16[128,2560]{1,0:T(8,128)(2,1)}, u32[]{:S(2)}, u32[]{:S(2)}) collective-permute-start(bf16[128,2560]{1,0:T(8,128)(2,1)} %collective-permute-done.refs_2_), channel_id=1, source_target_pairs={{0,1},{1,0},{2,3},{3,2},{4,5},{5,4},{6,7},{7,6},{8,9},{9,8},{10,11... | collective-permute-start | bytes 1966088 | tf_op jit(solution)/shard_map/ppermute | solution.py:29
  42.0 36.4 %collective-permute-start.8 = (bf16[128,2560]{1,0:T(8,128)(2,1)}, bf16[128,2560]{1,0:T(8,128)(2,1)}, u32[]{:S(2)}, u32[]{:S(2)}) collective-permute-start(bf16[128,2560]{1,0:T(8,128)(2,1)} %collective-permute-done.1.refs_4_), channel_id=1, source_target_pairs={{0,1},{1,0},{2,3},{3,2},{4,5},{5,4},{6,7},{7,6},{8,9},{9,8},{10,11... | collective-permute-start | bytes 1966088 | tf_op jit(solution)/shard_map/ppermute | solution.py:29
  52.4 26.0 %collective-permute-start.10 = (bf16[128,2560]{1,0:T(8,128)(2,1)}, bf16[128,2560]{1,0:T(8,128)(2,1)}, u32[]{:S(2)}, u32[]{:S(2)}) collective-permute-start(bf16[128,2560]{1,0:T(8,128)(2,1)} %collective-permute-done.9.refs_6_), channel_id=1, source_target_pairs={{0,1},{1,0},{2,3},{3,2},{4,5},{5,4},{6,7},{7,6},{8,9},{9,8},{10,11... | collective-permute-start | bytes 1966088 | tf_op jit(solution)/shard_map/ppermute | solution.py:29
  66.4 28.1 %collective-permute-start.3 = (bf16[128,2560]{1,0:T(8,128)(2,1)}, bf16[128,2560]{1,0:T(8,128)(2,1)}, u32[]{:S(2)}, u32[]{:S(2)}) collective-permute-start(bf16[128,2560]{1,0:T(8,128)(2,1)} %collective-permute-done.2.refs_2_), channel_id=1, source_target_pairs={{0,2},{2,4},{4,6},{6,0},{1,3},{3,5},{5,7},{7,1},{8,10},{10,12},{12... | collective-permute-start | bytes 1966088 | tf_op jit(solution)/shard_map/ppermute | solution.py:354
  85.0 41.2 %all-to-all-start.1 = ((bf16[16,160,384]{2,1,0:T(8,128)(2,1)}), bf16[16,160,384]{2,1,0:T(8,128)(2,1)}, u32[]{:S(2)}, u32[]{:S(2)}) async-start(bf16[16,160,384]{2,1,0:T(8,128)(2,1)} %bitcast.6), calls=%async_computation.1 | async-start | bytes 3932160 | tf_op jit(solution)/shard_map/all_to_all | solution.py:377
  94.6 15.2 %collective-permute-start.4 = (bf16[128,2560]{1,0:T(8,128)(2,1)}, bf16[128,2560]{1,0:T(8,128)(2,1)S(1)}, u32[]{:S(2)}, u32[]{:S(2)}) collective-permute-start(bf16[128,2560]{1,0:T(8,128)(2,1)} %collective-permute-done.3.refs_4_), channel_id=1, source_target_pairs={{0,2},{2,4},{4,6},{6,0},{1,3},{3,5},{5,7},{7,1},{8,10},{10,12},{12... | collective-permute-start | bytes 1966088 | tf_op jit(solution)/shard_map/ppermute | solution.py:354
  94.7 19.1 %collective-permute-start.11 = (bf16[128,2560]{1,0:T(8,128)(2,1)}, bf16[128,2560]{1,0:T(8,128)(2,1)S(1)}, u32[]{:S(2)}, u32[]{:S(2)}) collective-permute-start(bf16[128,2560]{1,0:T(8,128)(2,1)} %collective-permute-done.2.refs_2_), channel_id=1, source_target_pairs={{0,1},{1,0},{2,3},{3,2},{4,5},{5,4},{6,7},{7,6},{8,9},{9,8},{10,11... | collective-permute-start | bytes 1966088 | tf_op jit(solution)/shard_map/ppermute | solution.py:29
  98.0 15.8 %collective-permute-start.12 = (bf16[128,2560]{1,0:T(8,128)(2,1)}, bf16[128,2560]{1,0:T(8,128)(2,1)S(1)}, u32[]{:S(2)}, u32[]{:S(2)}) collective-permute-start(bf16[128,2560]{1,0:T(8,128)(2,1)} %collective-permute-done.3.refs_4_), channel_id=1, source_target_pairs={{0,1},{1,0},{2,3},{3,2},{4,5},{5,4},{6,7},{7,6},{8,9},{9,8},{10,11... | collective-permute-start | bytes 1966088 | tf_op jit(solution)/shard_map/ppermute | solution.py:29
  109.8 5.7 %collective-permute-start.5 = (bf16[128,2560]{1,0:T(8,128)(2,1)S(1)}, bf16[128,2560]{1,0:T(8,128)(2,1)S(1)}, u32[]{:S(2)}, u32[]{:S(2)}) collective-permute-start(bf16[128,2560]{1,0:T(8,128)(2,1)S(1)} %collective-permute-done.4.refs_0_.refs_6_), channel_id=1, source_target_pairs={{0,1},{1,0},{2,3},{3,2},{4,5},{5,4},{6,7},{7,6},{8,9},{9,8},{10,11... | collective-permute-start | bytes 1966088 | tf_op jit(solution)/shard_map/ppermute | solution.py:29
  126.2 38.3 %all-to-all-start = ((bf16[16,160,384]{2,1,0:T(8,128)(2,1)}), bf16[16,160,384]{2,1,0:T(8,128)(2,1)}, u32[]{:S(2)}, u32[]{:S(2)}) async-start(bf16[16,160,384]{2,1,0:T(8,128)(2,1)} %bitcast.5), calls=%async_computation | async-start | bytes 3932160 | tf_op jit(solution)/shard_map/all_to_all | solution.py:377
  132.8 5.9 %copy-start.17 = (bf16[128,2560]{1,0:T(8,128)(2,1)S(1)}, bf16[128,2560]{1,0:T(8,128)(2,1)}, u32[]{:S(2)}) copy-start(bf16[128,2560]{1,0:T(8,128)(2,1)} %copy-done.16) | copy-start | bytes 1966084
  132.9 5.9 %copy-start.19 = (bf16[128,2560]{1,0:T(8,128)(2,1)S(1)}, bf16[128,2560]{1,0:T(8,128)(2,1)}, u32[]{:S(2)}) copy-start(bf16[128,2560]{1,0:T(8,128)(2,1)} %copy-done.18) | copy-start | bytes 1966084
  153.4 40.9 %collective-permute-start.13 = (bf16[3,512,256]{2,1,0:T(8,128)(2,1)S(1)}, bf16[3,512,256]{2,1,0:T(8,128)(2,1)S(1)}, u32[]{:S(2)}, u32[]{:S(2)}) collective-permute-start(bf16[3,512,256]{2,1,0:T(8,128)(2,1)S(1)} %get-tuple-element.35), channel_id=1, source_target_pairs={{0,128},{128,0},{1,129},{129,1},{2,130},{130,2},{3,131},{131,3},{4... | collective-permute-start | bytes 2359304 | tf_op jit(solution)/shard_map/ppermute | solution.py:29
  162.2 50.4 %collective-permute-start.14 = (bf16[3,512,128]{2,1,0:T(8,128)(2,1)S(1)}, bf16[3,512,128]{2,1,0:T(8,128)(2,1)S(1)}, u32[]{:S(2)}, u32[]{:S(2)}) collective-permute-start(bf16[3,512,128]{2,1,0:T(8,128)(2,1)S(1)} %get-tuple-element.39), channel_id=1, source_target_pairs={{0,128},{128,0},{1,129},{129,1},{2,130},{130,2},{3,131},{131,3},{4... | collective-permute-start | bytes 1179656 | tf_op jit(solution)/shard_map/ppermute | solution.py:29
  164.5 29.8 %copy-start.22 = (s32[32]{0:T(128)S(1)}, s32[32]{0:T(128)}, u32[]{:S(2)}) copy-start(s32[32]{0:T(128)} %counts_ref.3) | copy-start | bytes 388
  166.4 48.9 %collective-permute-start.15 = (bf16[160,384]{1,0:T(8,128)(2,1)S(1)}, bf16[160,384]{1,0:T(8,128)(2,1)S(1)}, u32[]{:S(2)}, u32[]{:S(2)}) collective-permute-start(bf16[160,384]{1,0:T(8,128)(2,1)S(1)} %select_convert_fusion), channel_id=1, source_target_pairs={{0,128},{128,0},{1,129},{129,1},{2,130},{130,2},{3,131},{131,3},{4... | collective-permute-start | bytes 368648 | tf_op jit(solution)/shard_map/ppermute | solution.py:29
  (19 other events, 41.2 us)

commit v3 on v2

--- a/solution.py
+++ b/solution.py
@@ -15,6 +15,7 @@
 MOVABLE = 4
 CHIPS = 4
 REPLICAS = 32
+ROOMY = 58
 SCALE = HEAD_SIZE**-0.5
 LOG2E = 1.4426950408889634
 DP = ("z_hi", "y", "x")
@@ -171,14 +172,14 @@
             out,
             jax.ShapeDtypeStruct((inner, rows), jnp.bfloat16),
         ],
-        compiler_params=room(20),
+        compiler_params=room(ROOMY),
         cost_estimate=cost(
             4 * rows * keys * inner,
             12 * rows * inner + 2 * heads * rows * keys,
             heads * rows * keys,
         ),
         name="forward",
-    )(here, ids, q, k, v)
+    )(here, ids, *map(in_hbm, (q, k, v)))
 
 
 def backward(here, ids, first, heads, q, kt, v, g, o, p, before):
@@ -201,13 +202,13 @@
         out_shape=[jax.ShapeDtypeStruct((rows, inner), jnp.bfloat16)] * 3
         + [jax.ShapeDtypeStruct((3, moving, heads * HEAD_SIZE), jnp.bfloat16)],
         input_output_aliases={8 + i: i for i in range(len(before))},
-        compiler_params=room(20),
+        compiler_params=room(ROOMY),
         cost_estimate=cost(
             8 * rows * keys * heads * HEAD_SIZE,
             19 * rows * heads * HEAD_SIZE + 2 * heads * rows * keys,
         ),
         name="backward",
-    )(here, ids, q, kt, v, g, o, p, *before)
+    )(here, ids, *map(in_hbm, (q, kt, v, g, o, p)), *before)
 
 
 def settle(here, counts, first, local, arrived):
@@ -277,14 +278,14 @@
     final = partial is not None
     in_specs = piece_specs(pieces, first, width)
     in_specs.append(pl.BlockSpec((inner, width), lambda j, *_: (0, at + j)))
-    operands = [*pieces, in_hbm(w)]
+    operands = [*map(in_hbm, pieces), in_hbm(w)]
     aliases = {}
     total = rows
     out_spec = pl.BlockSpec((rows, inner), lambda j, *_: (0, 0))
     if final:
         total = partial.shape[0]
         in_specs.append(pl.BlockSpec((rows, inner), lambda j, *_: (place, 0)))
-        operands.append(partial)
+        operands.append(in_hbm(partial))
         out_spec = pl.BlockSpec((total, inner), lambda j, *_: (0, 0))
     if before is not None:
         in_specs.append(ANY)
@@ -300,7 +301,7 @@
         ),
         out_shape=jax.ShapeDtypeStruct((total, inner), jnp.bfloat16 if final else jnp.float32),
         input_output_aliases=aliases,
-        compiler_params=room(30),
+        compiler_params=room(ROOMY),
         cost_estimate=cost(
             2 * rows * depth * inner, 2 * rows * depth + 2 * inner * depth + 8 * rows * inner
         ),
@@ -328,12 +329,12 @@
             pl.BlockSpec((width, inner), lambda j, *_: (j, 0)),
         ),
         out_shape=jax.ShapeDtypeStruct((depth, inner), jnp.bfloat16),
-        compiler_params=room(26),
+        compiler_params=room(ROOMY),
         cost_estimate=cost(
             2 * rows * depth * inner, 2 * rows * depth + 2 * depth * inner + 2 * rows * inner
         ),
         name="weight",
-    )(here, *pieces, h)
+    )(here, *map(in_hbm, pieces), h)
 
 
 def after(x, *others):

time: 217 us -> 218 us (level)
  Pallas kernels: 43.3 us -> 56.6 us
  local copies, waits for them, and re-layouts: 16.1 us -> 5.91 us
    unnamed x51 -> x23, local copies, waits for them, and re-layouts: 13 us -> 2.57 us
    pallas_call x3, Pallas kernels: 13.9 us -> 18.2 us  [project(): pl.pallas_call(functools.partial(project_kernel, turns, final), grid_spec...]
    pallas_call x2, Pallas kernels: 10.1 us -> 14.1 us  [weight(): pl.pallas_call(weight_kernel, grid_spec=prefetched(1, (depth // width,),...]
    pallas_call x2, Pallas kernels: 10.3 us -> 13.5 us  [backward(): pl.pallas_call(backward_kernel, grid_spec=prefetched(2, (heads,), [hs, ts...]
  transfers between devices with their start and end apart: 18 -> 18, of which waited for: 9 -> 9; matrix products, arithmetic and copies ran while one was open for 3% -> 3% of each run, Pallas kernels for 20% -> 26%
where the time goes in v3:
time: 218 us; the launch traced here: 217 us
  waiting for transfers between devices  101 us (46%)
  Pallas kernels  56.6 us (26%)
  starting transfers between devices  49.3 us (23%)
  local copies, waits for them, and re-layouts  5.91 us (3%)
  other arithmetic  3.52 us (2%)
    ppermute x6, waiting for transfers between devices, turn(): y = lax.ppermute(x, 'z_lo', ring)  58.3 us
    ppermute x10, waiting for transfers between devices, swapped(): return lax.ppermute(x, axis, [(i, (i + n // 2) % n) for i in range(n)])  42.6 us
    ppermute x10, starting transfers between devices, swapped(): return lax.ppermute(x, axis, [(i, (i + n // 2) % n) for i in range(n)])  30.5 us
    pallas_call x3, Pallas kernels, project(): pl.pallas_call(functools.partial(project_kernel, turns, final), grid_spec...  18.2 us
    all_to_all x2, starting transfers between devices, steps(): tiles = lax.all_to_all(tiles, ('y', 'x'), 0, 0, tiled=True)  16.2 us
    pallas_call x2, Pallas kernels, weight(): pl.pallas_call(weight_kernel, grid_spec=prefetched(1, (depth // width,),...  14.1 us
    pallas_call x2, Pallas kernels, backward(): pl.pallas_call(backward_kernel, grid_spec=prefetched(2, (heads,), [hs, ts...  13.5 us
    pallas_call x1, Pallas kernels, forward(): pl.pallas_call(forward_kernel, grid_spec=prefetched(2, (heads,), [hs] * 3...  7.85 us
  transfers between devices with their start and end apart: 18, of which 9 were waited for; matrix products, arithmetic and copies ran while one was open for 3% of the time, Pallas kernels for 26%

profile of v3, /device:TPU:1, one launch (start us, length us, event | category | flops | bytes accessed | tf_op | source)
XLA Modules:
  0.0 217.1 jit_solution(5237551999066817212)
XLA Ops:
  1.8 2.5 %collective-permute-start = (bf16[128,2560]{1,0:T(8,128)(2,1)S(1)}, bf16[128,2560]{1,0:T(8,128)(2,1)S(1)}, u32[]{:S(2)}, u32[]{:S(2)}) collective-permute-start(bf16[128,2560]{1,0:T(8,128)(2,1)S(1)} %slice.6), channel_id=1, source_target_pairs={{0,2},{2,4},{4,6},{6,0},{1,3},{3,5},{5,7},{7,1},{8,10},{10,12},{12... | collective-permute-start | bytes 1966088 | tf_op jit(solution)/shard_map/ppermute | solution.py:355
  4.3 16.2 %collective-permute-done.refs_2_ = bf16[128,2560]{1,0:T(8,128)(2,1)S(1)} collective-permute-done((bf16[128,2560]{1,0:T(8,128)(2,1)S(1)}, bf16[128,2560]{1,0:T(8,128)(2,1)S(1)}, u32[]{:S(2)}, u32[]{:S(2)}) %collective-permute-start) | collective-permute-done | bytes 655392 | tf_op jit(solution)/shard_map/ppermute | solution.py:355
  22.7 13.8 %collective-permute-done.1.refs_4_ = bf16[128,2560]{1,0:T(8,128)(2,1)S(1)} collective-permute-done((bf16[128,2560]{1,0:T(8,128)(2,1)S(1)}, bf16[128,2560]{1,0:T(8,128)(2,1)S(1)}, u32[]{:S(2)}, u32[]{:S(2)}) %collective-permute-start.1) | collective-permute-done | bytes 655392 | tf_op jit(solution)/shard_map/ppermute | solution.py:355
  38.7 3.0 %collective-permute-start.7 = (bf16[128,2560]{1,0:T(8,128)(2,1)S(1)}, bf16[128,2560]{1,0:T(8,128)(2,1)}, u32[]{:S(2)}, u32[]{:S(2)}) collective-permute-start(bf16[128,2560]{1,0:T(8,128)(2,1)S(1)} %collective-permute-done.refs_2_), channel_id=1, source_target_pairs={{0,1},{1,0},{2,3},{3,2},{4,5},{5,4},{6,7},{7,6},{8,9},{9,8},{10,11... | collective-permute-start | bytes 1966088 | tf_op jit(solution)/shard_map/ppermute | solution.py:30
  41.7 9.9 %collective-permute-done.9.refs_6_ = bf16[128,2560]{1,0:T(8,128)(2,1)S(1)} collective-permute-done((bf16[128,2560]{1,0:T(8,128)(2,1)S(1)}, bf16[128,2560]{1,0:T(8,128)(2,1)S(1)}, u32[]{:S(2)}, u32[]{:S(2)}) %collective-permute-start.9) | collective-permute-done | bytes 655392 | tf_op jit(solution)/shard_map/ppermute | solution.py:355
  51.6 7.3 %collective-permute-start.10 = (bf16[128,2560]{1,0:T(8,128)(2,1)S(1)}, bf16[128,2560]{1,0:T(8,128)(2,1)}, u32[]{:S(2)}, u32[]{:S(2)}) collective-permute-start(bf16[128,2560]{1,0:T(8,128)(2,1)S(1)} %collective-permute-done.9.refs_6_), channel_id=1, source_target_pairs={{0,1},{1,0},{2,3},{3,2},{4,5},{5,4},{6,7},{7,6},{8,9},{9,8},{10,11... | collective-permute-start | bytes 1966088 | tf_op jit(solution)/shard_map/ppermute | solution.py:30
  58.9 6.8 %collective-permute-done.2.refs_2_ = bf16[128,2560]{1,0:T(8,128)(2,1)} collective-permute-done((bf16[128,2560]{1,0:T(8,128)(2,1)}, bf16[128,2560]{1,0:T(8,128)(2,1)}, u32[]{:S(2)}, u32[]{:S(2)}) %collective-permute-start.2) | collective-permute-done | bytes 655392 | tf_op jit(solution)/shard_map/ppermute | solution.py:355
  67.0 7.9 %forward.1 = (bf16[3,8,512,128]{3,2,1,0:T(8,128)(2,1)}, bf16[1024,384]{1,0:T(8,128)(2,1)}, bf16[1024,384]{1,0:T(8,128)(2,1)}, bf16[384,1024]{1,0:T(8,128)(2,1)}) custom-call(s32[3]{0:T(128)} %pad_add_fusion.here_ref, s32[32,8]{1,0:T(8,128)} %copy.23.ids_ref, bf16[1024,384]{1,0:T(8,128)(2,1)} %q_ref.5, bf16[1024,384]{1,0:T(8,128)(2,1)} %k_ref.1, ...), custom_call_target="tpu_custom_call" | custom-call | flops 805306368 | bytes 7864320 | tf_op jit(solution)/shard_map/forward/pallas_call | solution.py:160
  76.0 7.1 %weight.3 = bf16[2560,384]{1,0:T(8,128)(2,1)} custom-call(s32[3]{0:T(128)} %pad_add_fusion.here_ref, bf16[128,5120]{1,0:T(8,128)(2,1)} %refs_0_.7, bf16[128,5120]{1,0:T(8,128)(2,1)} %copy-done.2, bf16[128,2560]{1,0:T(8,128)(2,1)} %copy-done.3, bf16[128,2560]{1,0:T(8,128)(2,1)} %collective-permute-done.7.refs_3_, bf16[128,2560]{1,0:T(8,128)(2,1)} %copy-done.4, ...), custom_call_target="tpu_custom_call" | custom-call | flops 2013265920 | bytes 7995392 | tf_op jit(solution)/shard_map/weight/pallas_call | solution.py:323
  83.1 9.5 %all-to-all-start.1 = ((bf16[16,160,384]{2,1,0:T(8,128)(2,1)}), bf16[16,160,384]{2,1,0:T(8,128)(2,1)S(1)}, u32[]{:S(2)}, u32[]{:S(2)}) async-start(bf16[16,160,384]{2,1,0:T(8,128)(2,1)} %bitcast.6), calls=%async_computation.1 | async-start | bytes 3932160 | tf_op jit(solution)/shard_map/all_to_all | solution.py:378
  92.7 3.3 %collective-permute-start.11 = (bf16[128,2560]{1,0:T(8,128)(2,1)}, bf16[128,2560]{1,0:T(8,128)(2,1)S(1)}, u32[]{:S(2)}, u32[]{:S(2)}) collective-permute-start(bf16[128,2560]{1,0:T(8,128)(2,1)} %collective-permute-done.2.refs_2_), channel_id=1, source_target_pairs={{0,1},{1,0},{2,3},{3,2},{4,5},{5,4},{6,7},{7,6},{8,9},{9,8},{10,11... | collective-permute-start | bytes 1966088 | tf_op jit(solution)/shard_map/ppermute | solution.py:30
  96.1 11.6 %collective-permute-done.4.refs_0_.refs_6_ = bf16[128,2560]{1,0:T(8,128)(2,1)S(1)} collective-permute-done((bf16[128,2560]{1,0:T(8,128)(2,1)}, bf16[128,2560]{1,0:T(8,128)(2,1)S(1)}, u32[]{:S(2)}, u32[]{:S(2)}) %collective-permute-start.4) | collective-permute-done | bytes 655392 | tf_op jit(solution)/shard_map/ppermute | solution.py:355
  107.7 4.1 %collective-permute-start.5 = (bf16[128,2560]{1,0:T(8,128)(2,1)S(1)}, bf16[128,2560]{1,0:T(8,128)(2,1)S(1)}, u32[]{:S(2)}, u32[]{:S(2)}) collective-permute-start(bf16[128,2560]{1,0:T(8,128)(2,1)S(1)} %collective-permute-done.4.refs_0_.refs_6_), channel_id=1, source_target_pairs={{0,1},{1,0},{2,3},{3,2},{4,5},{5,4},{6,7},{7,6},{8,9},{9,8},{10,11... | collective-permute-start | bytes 1966088 | tf_op jit(solution)/shard_map/ppermute | solution.py:30
  114.4 7.0 %weight.2 = bf16[2560,384]{1,0:T(8,128)(2,1)} custom-call(s32[3]{0:T(128)} %pad_add_fusion.here_ref, bf16[128,5120]{1,0:T(8,128)(2,1)} %refs_0_.7, bf16[128,5120]{1,0:T(8,128)(2,1)} %copy-done.2, bf16[128,2560]{1,0:T(8,128)(2,1)} %collective-permute-done.2.refs_2_, bf16[128,2560]{1,0:T(8,128)(2,1)} %copy-done.7, ...), custom_call_target="tpu_custom_call" | custom-call | flops 2013265920 | bytes 7995392 | tf_op jit(solution)/shard_map/weight/pallas_call | solution.py:323
  121.4 6.7 %all-to-all-start = ((bf16[16,160,384]{2,1,0:T(8,128)(2,1)}), bf16[16,160,384]{2,1,0:T(8,128)(2,1)}, u32[]{:S(2)}, u32[]{:S(2)}) async-start(bf16[16,160,384]{2,1,0:T(8,128)(2,1)} %bitcast.5), calls=%async_computation | async-start | bytes 3932160 | tf_op jit(solution)/shard_map/all_to_all | solution.py:378
  128.2 7.3 %project.3.refs_7_.refs_3_ = f32[1024,384]{1,0:T(8,128)} custom-call(s32[3]{0:T(128)} %pad_add_fusion.here_ref, bf16[128,5120]{1,0:T(8,128)(2,1)} %refs_0_.7, bf16[128,5120]{1,0:T(8,128)(2,1)} %copy-done.2, bf16[128,2560]{1,0:T(8,128)(2,1)} %copy-done.3, bf16[128,2560]{1,0:T(8,128)(2,1)} %collective-permute-done.7.refs_3_, bf16[128,2560]{1,0:T(8,128)(2,1)} %copy-done.4, ...), custom_call_target="tpu_custom_call" | custom-call | flops 2013265920 | bytes 10354688 | tf_op jit(solution)/shard_map/project/pallas_call | solution.py:297
  135.5 6.8 %project.4.refs_4_ = bf16[1024,384]{1,0:T(8,128)(2,1)} custom-call(s32[3]{0:T(128)} %pad_add_fusion.here_ref, bf16[128,5120]{1,0:T(8,128)(2,1)} %refs_0_.7, bf16[128,5120]{1,0:T(8,128)(2,1)} %copy-done.2, bf16[128,2560]{1,0:T(8,128)(2,1)} %collective-permute-done.2.refs_2_, bf16[128,2560]{1,0:T(8,128)(2,1)} %copy-done.7, ...), custom_call_target="tpu_custom_call" | custom-call | flops 1509949440 | bytes 8257536 | tf_op jit(solution)/shard_map/project/pallas_call | solution.py:297
  142.3 4.1 %project.5.g_ref = bf16[1024,384]{1,0:T(8,128)(2,1)} custom-call(s32[3]{0:T(128)} %pad_add_fusion.here_ref, bf16[128,2560]{1,0:T(8,128)(2,1)} %copy-done.6, bf16[128,2560]{1,0:T(8,128)(2,1)} %copy-done.9, bf16[384,5120]{1,0:T(8,128)(2,1)} %refs_2_.1, f32[1024,384]{1,0:T(8,128)} %project.3.refs_7_.refs_3_, ...), custom_call_target="tpu_custom_call", output_to_operand_aliasing={{}: (5, {})} | custom-call | flops 503316480 | bytes 4063232 | tf_op jit(solution)/shard_map/project/pallas_call | solution.py:297
  146.4 7.8 %backward.2 = (bf16[1024,384]{1,0:T(8,128)(2,1)}, bf16[1024,384]{1,0:T(8,128)(2,1)}, bf16[1024,384]{1,0:T(8,128)(2,1)}, bf16[3,512,256]{2,1,0:T(8,128)(2,1)}) custom-call(s32[3]{0:T(128)} %pad_add_fusion.here_ref, s32[32,8]{1,0:T(8,128)} %copy.23.ids_ref, bf16[1024,384]{1,0:T(8,128)(2,1)} %q_ref.5, bf16[384,1024]{1,0:T(8,128)(2,1)} %get-tuple-element.24.kt_ref, ...), custom_call_target="tpu_custom_call" | custom-call | flops 1073741824 | bytes 7077888 | tf_op jit(solution)/shard_map/backward/pallas_call | solution.py:193
  154.2 5.0 %collective-permute-start.13 = (bf16[3,512,256]{2,1,0:T(8,128)(2,1)}, bf16[3,512,256]{2,1,0:T(8,128)(2,1)S(1)}, u32[]{:S(2)}, u32[]{:S(2)}) collective-permute-start(bf16[3,512,256]{2,1,0:T(8,128)(2,1)} %get-tuple-element.35), channel_id=1, source_target_pairs={{0,128},{128,0},{1,129},{129,1},{2,130},{130,2},{3,131},{131,3},{4... | collective-permute-start | bytes 2359304 | tf_op jit(solution)/shard_map/ppermute | solution.py:30
  159.3 5.6 %backward.3 = (bf16[1024,384]{1,0:T(8,128)(2,1)}, bf16[1024,384]{1,0:T(8,128)(2,1)}, bf16[1024,384]{1,0:T(8,128)(2,1)}, bf16[3,512,128]{2,1,0:T(8,128)(2,1)}) custom-call(s32[3]{0:T(128)} %pad_add_fusion.here_ref, s32[32,8]{1,0:T(8,128)} %copy.23.ids_ref, bf16[1024,384]{1,0:T(8,128)(2,1)} %q_ref.5, ...), custom_call_target="tpu_custom_call", output_to_operand_aliasing={{0}: (8, {}), {1}: (9, {}), {2}: (10, {})} | custom-call | flops 536870912 | bytes 3538944 | tf_op jit(solution)/shard_map/backward/pallas_call | solution.py:193
  167.5 5.1 %collective-permute-start.15 = (bf16[160,384]{1,0:T(8,128)(2,1)S(1)}, bf16[160,384]{1,0:T(8,128)(2,1)S(1)}, u32[]{:S(2)}, u32[]{:S(2)}) collective-permute-start(bf16[160,384]{1,0:T(8,128)(2,1)S(1)} %select_convert_fusion), channel_id=1, source_target_pairs={{0,128},{128,0},{1,129},{129,1},{2,130},{130,2},{3,131},{131,3},{4... | collective-permute-start | bytes 368648 | tf_op jit(solution)/shard_map/ppermute | solution.py:30
  172.5 22.2 %collective-permute-done.13.refs_3_ = bf16[3,512,256]{2,1,0:T(8,128)(2,1)S(1)} collective-permute-done((bf16[3,512,256]{2,1,0:T(8,128)(2,1)}, bf16[3,512,256]{2,1,0:T(8,128)(2,1)S(1)}, u32[]{:S(2)}, u32[]{:S(2)}) %collective-permute-start.13) | collective-permute-done | bytes 786464 | tf_op jit(solution)/shard_map/ppermute | solution.py:30
  196.3 17.4 %collective-permute-done.14.refs_3_ = bf16[3,512,128]{2,1,0:T(8,128)(2,1)S(1)} collective-permute-done((bf16[3,512,128]{2,1,0:T(8,128)(2,1)}, bf16[3,512,128]{2,1,0:T(8,128)(2,1)S(1)}, u32[]{:S(2)}, u32[]{:S(2)}) %collective-permute-start.14) | collective-permute-done | bytes 393248 | tf_op jit(solution)/shard_map/ppermute | solution.py:30
  (52 shorter events, 18.0 us)
Async XLA Ops:
  0.6 65.7 %copy-start.10 = (s32[32,8]{0,1:T(8,128)S(1)}, s32[32,8]{0,1:T(8,128)}, u32[]{:S(2)}) copy-start(s32[32,8]{0,1:T(8,128)} %param.12) | copy-start | bytes 3076
  1.8 18.8 %collective-permute-start = (bf16[128,2560]{1,0:T(8,128)(2,1)S(1)}, bf16[128,2560]{1,0:T(8,128)(2,1)S(1)}, u32[]{:S(2)}, u32[]{:S(2)}) collective-permute-start(bf16[128,2560]{1,0:T(8,128)(2,1)S(1)} %slice.6), channel_id=1, source_target_pairs={{0,2},{2,4},{4,6},{6,0},{1,3},{3,5},{5,7},{7,1},{8,10},{10,12},{12... | collective-permute-start | bytes 1966088 | tf_op jit(solution)/shard_map/ppermute | solution.py:355
  20.6 54.3 %copy-start.3 = (bf16[128,2560]{1,0:T(8,128)(2,1)}, bf16[128,2560]{1,0:T(8,128)(2,1)S(1)}, u32[]{:S(2)}) copy-start(bf16[128,2560]{1,0:T(8,128)(2,1)S(1)} %collective-permute-done.refs_2_) | copy-start | bytes 1966084
  20.6 15.9 %collective-permute-start.1 = (bf16[128,2560]{1,0:T(8,128)(2,1)S(1)}, bf16[128,2560]{1,0:T(8,128)(2,1)S(1)}, u32[]{:S(2)}, u32[]{:S(2)}) collective-permute-start(bf16[128,2560]{1,0:T(8,128)(2,1)S(1)} %collective-permute-done.refs_2_), channel_id=1, source_target_pairs={{0,2},{2,4},{4,6},{6,0},{1,3},{3,5},{5,7},{7,1},{8,10},{10,12},{12... | collective-permute-start | bytes 1966088 | tf_op jit(solution)/shard_map/ppermute | solution.py:355
  20.6 54.4 %collective-permute-start.6 = (bf16[128,5120]{1,0:T(8,128)(2,1)}, bf16[128,5120]{1,0:T(8,128)(2,1)S(1)}, u32[]{:S(2)}, u32[]{:S(2)}) collective-permute-start(bf16[128,5120]{1,0:T(8,128)(2,1)} %refs_0_.7), channel_id=1, source_target_pairs={{0,1},{1,0},{2,3},{3,2},{4,5},{5,4},{6,7},{7,6},{8,9},{9,8},{10,11... | collective-permute-start | bytes 3932168 | tf_op jit(solution)/shard_map/ppermute | solution.py:30
  36.5 38.4 %copy-start.4 = (bf16[128,2560]{1,0:T(8,128)(2,1)}, bf16[128,2560]{1,0:T(8,128)(2,1)S(1)}, u32[]{:S(2)}) copy-start(bf16[128,2560]{1,0:T(8,128)(2,1)S(1)} %collective-permute-done.1.refs_4_) | copy-start | bytes 1966084
  36.5 15.1 %collective-permute-start.9 = (bf16[128,2560]{1,0:T(8,128)(2,1)S(1)}, bf16[128,2560]{1,0:T(8,128)(2,1)S(1)}, u32[]{:S(2)}, u32[]{:S(2)}) collective-permute-start(bf16[128,2560]{1,0:T(8,128)(2,1)S(1)} %collective-permute-done.1.refs_4_), channel_id=1, source_target_pairs={{0,2},{2,4},{4,6},{6,0},{1,3},{3,5},{5,7},{7,1},{8,10},{10,12},{12... | collective-permute-start | bytes 1966088 | tf_op jit(solution)/shard_map/ppermute | solution.py:355
  38.7 27.0 %collective-permute-start.2 = (bf16[128,2560]{1,0:T(8,128)(2,1)}, bf16[128,2560]{1,0:T(8,128)(2,1)}, u32[]{:S(2)}, u32[]{:S(2)}) collective-permute-start(bf16[128,2560]{1,0:T(8,128)(2,1)} %slice.7), channel_id=1, source_target_pairs={{0,2},{2,4},{4,6},{6,0},{1,3},{3,5},{5,7},{7,1},{8,10},{10,12},{12... | collective-permute-start | bytes 1966088 | tf_op jit(solution)/shard_map/ppermute | solution.py:355
  38.7 36.2 %collective-permute-start.7 = (bf16[128,2560]{1,0:T(8,128)(2,1)S(1)}, bf16[128,2560]{1,0:T(8,128)(2,1)}, u32[]{:S(2)}, u32[]{:S(2)}) collective-permute-start(bf16[128,2560]{1,0:T(8,128)(2,1)S(1)} %collective-permute-done.refs_2_), channel_id=1, source_target_pairs={{0,1},{1,0},{2,3},{3,2},{4,5},{5,4},{6,7},{7,6},{8,9},{9,8},{10,11... | collective-permute-start | bytes 1966088 | tf_op jit(solution)/shard_map/ppermute | solution.py:30
  41.7 33.2 %collective-permute-start.8 = (bf16[128,2560]{1,0:T(8,128)(2,1)S(1)}, bf16[128,2560]{1,0:T(8,128)(2,1)}, u32[]{:S(2)}, u32[]{:S(2)}) collective-permute-start(bf16[128,2560]{1,0:T(8,128)(2,1)S(1)} %collective-permute-done.1.refs_4_), channel_id=1, source_target_pairs={{0,1},{1,0},{2,3},{3,2},{4,5},{5,4},{6,7},{7,6},{8,9},{9,8},{10,11... | collective-permute-start | bytes 1966088 | tf_op jit(solution)/shard_map/ppermute | solution.py:30
  51.6 23.4 %copy-start.5 = (bf16[128,2560]{1,0:T(8,128)(2,1)}, bf16[128,2560]{1,0:T(8,128)(2,1)S(1)}, u32[]{:S(2)}) copy-start(bf16[128,2560]{1,0:T(8,128)(2,1)S(1)} %collective-permute-done.9.refs_6_) | copy-start | bytes 1966084
  51.6 23.4 %collective-permute-start.10 = (bf16[128,2560]{1,0:T(8,128)(2,1)S(1)}, bf16[128,2560]{1,0:T(8,128)(2,1)}, u32[]{:S(2)}, u32[]{:S(2)}) collective-permute-start(bf16[128,2560]{1,0:T(8,128)(2,1)S(1)} %collective-permute-done.9.refs_6_), channel_id=1, source_target_pairs={{0,1},{1,0},{2,3},{3,2},{4,5},{5,4},{6,7},{7,6},{8,9},{9,8},{10,11... | collective-permute-start | bytes 1966088 | tf_op jit(solution)/shard_map/ppermute | solution.py:30
  65.7 26.8 %collective-permute-start.3 = (bf16[128,2560]{1,0:T(8,128)(2,1)}, bf16[128,2560]{1,0:T(8,128)(2,1)}, u32[]{:S(2)}, u32[]{:S(2)}) collective-permute-start(bf16[128,2560]{1,0:T(8,128)(2,1)} %collective-permute-done.2.refs_2_), channel_id=1, source_target_pairs={{0,2},{2,4},{4,6},{6,0},{1,3},{3,5},{5,7},{7,1},{8,10},{10,12},{12... | collective-permute-start | bytes 1966088 | tf_op jit(solution)/shard_map/ppermute | solution.py:355
  83.1 38.3 %all-to-all-start.1 = ((bf16[16,160,384]{2,1,0:T(8,128)(2,1)}), bf16[16,160,384]{2,1,0:T(8,128)(2,1)S(1)}, u32[]{:S(2)}, u32[]{:S(2)}) async-start(bf16[16,160,384]{2,1,0:T(8,128)(2,1)} %bitcast.6), calls=%async_computation.1 | async-start | bytes 3932160 | tf_op jit(solution)/shard_map/all_to_all | solution.py:378
  92.6 15.1 %collective-permute-start.4 = (bf16[128,2560]{1,0:T(8,128)(2,1)}, bf16[128,2560]{1,0:T(8,128)(2,1)S(1)}, u32[]{:S(2)}, u32[]{:S(2)}) collective-permute-start(bf16[128,2560]{1,0:T(8,128)(2,1)} %collective-permute-done.3.refs_4_), channel_id=1, source_target_pairs={{0,2},{2,4},{4,6},{6,0},{1,3},{3,5},{5,7},{7,1},{8,10},{10,12},{12... | collective-permute-start | bytes 1966088 | tf_op jit(solution)/shard_map/ppermute | solution.py:355
  92.7 19.2 %collective-permute-start.11 = (bf16[128,2560]{1,0:T(8,128)(2,1)}, bf16[128,2560]{1,0:T(8,128)(2,1)S(1)}, u32[]{:S(2)}, u32[]{:S(2)}) collective-permute-start(bf16[128,2560]{1,0:T(8,128)(2,1)} %collective-permute-done.2.refs_2_), channel_id=1, source_target_pairs={{0,1},{1,0},{2,3},{3,2},{4,5},{5,4},{6,7},{7,6},{8,9},{9,8},{10,11... | collective-permute-start | bytes 1966088 | tf_op jit(solution)/shard_map/ppermute | solution.py:30
  96.0 15.8 %collective-permute-start.12 = (bf16[128,2560]{1,0:T(8,128)(2,1)}, bf16[128,2560]{1,0:T(8,128)(2,1)S(1)}, u32[]{:S(2)}, u32[]{:S(2)}) collective-permute-start(bf16[128,2560]{1,0:T(8,128)(2,1)} %collective-permute-done.3.refs_4_), channel_id=1, source_target_pairs={{0,1},{1,0},{2,3},{3,2},{4,5},{5,4},{6,7},{7,6},{8,9},{9,8},{10,11... | collective-permute-start | bytes 1966088 | tf_op jit(solution)/shard_map/ppermute | solution.py:30
  107.7 5.8 %collective-permute-start.5 = (bf16[128,2560]{1,0:T(8,128)(2,1)S(1)}, bf16[128,2560]{1,0:T(8,128)(2,1)S(1)}, u32[]{:S(2)}, u32[]{:S(2)}) collective-permute-start(bf16[128,2560]{1,0:T(8,128)(2,1)S(1)} %collective-permute-done.4.refs_0_.refs_6_), channel_id=1, source_target_pairs={{0,1},{1,0},{2,3},{3,2},{4,5},{5,4},{6,7},{7,6},{8,9},{9,8},{10,11... | collective-permute-start | bytes 1966088 | tf_op jit(solution)/shard_map/ppermute | solution.py:30
  121.4 44.1 %all-to-all-start = ((bf16[16,160,384]{2,1,0:T(8,128)(2,1)}), bf16[16,160,384]{2,1,0:T(8,128)(2,1)}, u32[]{:S(2)}, u32[]{:S(2)}) async-start(bf16[16,160,384]{2,1,0:T(8,128)(2,1)} %bitcast.5), calls=%async_computation | async-start | bytes 3932160 | tf_op jit(solution)/shard_map/all_to_all | solution.py:378
  154.2 40.5 %collective-permute-start.13 = (bf16[3,512,256]{2,1,0:T(8,128)(2,1)}, bf16[3,512,256]{2,1,0:T(8,128)(2,1)S(1)}, u32[]{:S(2)}, u32[]{:S(2)}) collective-permute-start(bf16[3,512,256]{2,1,0:T(8,128)(2,1)} %get-tuple-element.35), channel_id=1, source_target_pairs={{0,128},{128,0},{1,129},{129,1},{2,130},{130,2},{3,131},{131,3},{4... | collective-permute-start | bytes 2359304 | tf_op jit(solution)/shard_map/ppermute | solution.py:30
  164.9 48.9 %collective-permute-start.14 = (bf16[3,512,128]{2,1,0:T(8,128)(2,1)}, bf16[3,512,128]{2,1,0:T(8,128)(2,1)S(1)}, u32[]{:S(2)}, u32[]{:S(2)}) collective-permute-start(bf16[3,512,128]{2,1,0:T(8,128)(2,1)} %get-tuple-element.39), channel_id=1, source_target_pairs={{0,128},{128,0},{1,129},{129,1},{2,130},{130,2},{3,131},{131,3},{4... | collective-permute-start | bytes 1179656 | tf_op jit(solution)/shard_map/ppermute | solution.py:30
  165.5 29.2 %copy-start = (s32[3]{0:T(128)S(1)}, s32[3]{0:T(128)}, u32[]{:S(2)}) copy-start(s32[3]{0:T(128)} %pad_add_fusion.here_ref) | copy-start | bytes 40
  165.5 29.2 %copy-start.1 = (s32[32]{0:T(128)S(1)}, s32[32]{0:T(128)}, u32[]{:S(2)}) copy-start(s32[32]{0:T(128)} %counts_ref.3) | copy-start | bytes 388
  167.5 48.9 %collective-permute-start.15 = (bf16[160,384]{1,0:T(8,128)(2,1)S(1)}, bf16[160,384]{1,0:T(8,128)(2,1)S(1)}, u32[]{:S(2)}, u32[]{:S(2)}) collective-permute-start(bf16[160,384]{1,0:T(8,128)(2,1)S(1)} %select_convert_fusion), channel_id=1, source_target_pairs={{0,128},{128,0},{1,129},{129,1},{2,130},{130,2},{3,131},{131,3},{4... | collective-permute-start | bytes 368648 | tf_op jit(solution)/shard_map/ppermute | solution.py:30
  (5 other events, 11.2 us)

commit v4 on v2

--- a/solution.py
+++ b/solution.py
@@ -80,11 +80,11 @@
 def backward_kernel(
     here_ref, ids_ref, q_ref, kt_ref, v_ref, g_ref, o_ref, p_ref, *rest
 ):
-    dq_ref, dk_ref, dv_ref, tail_ref, ka, va = rest[-6:]
+    dq_ref, dk_ref, dv_ref, tail_ref, both = rest[-5:]
     row = here_ref[0]
     front = dq_ref.shape[0] - tail_ref.shape[1]
-    ka[...] = jnp.zeros_like(ka)
-    va[...] = jnp.zeros_like(va)
+    both[...] = jnp.zeros_like(both)
+    none = jnp.zeros((BLOCK, HEAD_SIZE), jnp.bfloat16)
     for b in range(ids_ref.shape[1]):
         _, _, near = window_of(ids_ref, row, b)
         rows = pl.ds(b * BLOCK, BLOCK)
@@ -96,10 +96,16 @@
         )
         ds = (p.astype(jnp.float32) * (dp - center)).astype(jnp.bfloat16)
         dq_ref[rows, :] = (dot(kt_ref[:, near], ds, (1, 0)) * SCALE).T.astype(jnp.bfloat16)
-        ka[near, :] += dot(ds, q_ref[rows, :], (1, 0))
-        va[near, :] += dot(p, g, (1, 0))
-    dk_ref[...] = (ka[...] * SCALE).astype(jnp.bfloat16)
-    dv_ref[...] = va[...].astype(jnp.bfloat16)
+        pair = jnp.concatenate(
+            [
+                jnp.concatenate([q_ref[rows, :], none], axis=1),
+                jnp.concatenate([none, g], axis=1),
+            ],
+            axis=0,
+        )
+        both[near, :] += dot(jnp.concatenate([ds, p], axis=1), pair, (1, 0))
+    dk_ref[...] = (both[:, :HEAD_SIZE] * SCALE).astype(jnp.bfloat16)
+    dv_ref[...] = both[:, HEAD_SIZE:].astype(jnp.bfloat16)
     for i, ref in enumerate((dq_ref, dk_ref, dv_ref)):
         tail_ref[i] = ref[front:, :]
 
@@ -196,7 +202,7 @@
             (heads,),
             [hs, ts, hs, hs, hs, ps] + [ANY] * len(before),
             [hs] * 3 + [pl.BlockSpec((3, moving, HEAD_SIZE), lambda h, *_: (0, 0, h))],
-            [pltpu.VMEM((rows, HEAD_SIZE), jnp.float32)] * 2,
+            [pltpu.VMEM((rows, 2 * HEAD_SIZE), jnp.float32)],
         ),
         out_shape=[jax.ShapeDtypeStruct((rows, inner), jnp.bfloat16)] * 3
         + [jax.ShapeDtypeStruct((3, moving, heads * HEAD_SIZE), jnp.bfloat16)],
@@ -298,7 +304,9 @@
         grid_spec=prefetched(
             1, (depth // width,), in_specs, out_spec, [pltpu.VMEM((rows, inner), jnp.float32)]
         ),
-        out_shape=jax.ShapeDtypeStruct((total, inner), jnp.bfloat16 if final else jnp.float32),
+        out_shape=jax.ShapeDtypeStruct((total, inner), jnp.bfloat16)
+        if final
+        else pltpu.HBM((total, inner), jnp.float32),
         input_output_aliases=aliases,
         compiler_params=room(30),
         cost_estimate=cost(
@@ -311,7 +319,8 @@
 def weight_kernel(here_ref, *refs):
     pieces, h_ref, out_ref = refs[: 2 * CHIPS], refs[2 * CHIPS], refs[-1]
     g = jnp.concatenate([ref[...] for ref in pieces], axis=0)
-    out_ref[...] = (dot(g, h_ref[...], (0, 0)) * (1.0 / REPLICAS)).astype(jnp.bfloat16)
+    term = (dot(g, h_ref[...], (0, 0)) * (1.0 / REPLICAS)).astype(jnp.bfloat16)
+    out_ref[...] = term.reshape(out_ref.shape)
 
 
 def weight(here, pieces, first, width, h):
@@ -325,9 +334,9 @@
             1,
             (depth // width,),
             in_specs,
-            pl.BlockSpec((width, inner), lambda j, *_: (j, 0)),
-        ),
-        out_shape=jax.ShapeDtypeStruct((depth, inner), jnp.bfloat16),
+            pl.BlockSpec((16 * width // depth, depth // 16, inner), lambda j, *_: (j, 0, 0)),
+        ),
+        out_shape=pltpu.HBM((16, depth // 16, inner), jnp.bfloat16),
         compiler_params=room(26),
         cost_estimate=cost(
             2 * rows * depth * inner, 2 * rows * depth + 2 * depth * inner + 2 * rows * inner
@@ -372,8 +381,7 @@
 
     sums = []
     for c in range(2):
-        term = weight(here, pieces[c], c * half, 1280, output_turned)
-        tiles = term.reshape(16, -1, term.shape[1])
+        tiles = weight(here, pieces[c], c * half, 1280, output_turned)
         tiles = lax.all_to_all(tiles, ("y", "x"), 0, 0, tiled=True)
         sums.append(jnp.sum(tiles.astype(jnp.float32), axis=0))
     upper = lax.axis_index("z_hi") == 1

time: 217 us -> 220 us (1.014)
  Pallas kernels: 43.3 us -> 47.4 us
    unnamed x51 -> x49, local copies, waits for them, and re-layouts: 13 us -> 12.6 us
  transfers between devices with their start and end apart: 18 -> 18, of which waited for: 9 -> 9; matrix products, arithmetic and copies ran while one was open for 3% -> 3% of each run, Pallas kernels for 20% -> 22%
where the time goes in v4:
time: 220 us; the launch traced here: 219 us
  waiting for transfers between devices  102 us (46%)
  starting transfers between devices  49.2 us (22%)
  Pallas kernels  47.4 us (22%)
  local copies, waits for them, and re-layouts  15.8 us (7%)
  other arithmetic  4.53 us (2%)
    ppermute x6, waiting for transfers between devices, turn(): y = lax.ppermute(x, 'z_lo', ring)  59.3 us
    ppermute x10, waiting for transfers between devices, swapped(): return lax.ppermute(x, axis, [(i, (i + n // 2) % n) for i in range(n)])  42.4 us
    ppermute x10, starting transfers between devices, swapped(): return lax.ppermute(x, axis, [(i, (i + n // 2) % n) for i in range(n)])  30.4 us
    all_to_all x2, starting transfers between devices, steps(): tiles = lax.all_to_all(tiles, ('y', 'x'), 0, 0, tiled=True)  16.2 us
    pallas_call x3, Pallas kernels, project(): pl.pallas_call(functools.partial(project_kernel, turns, final), grid_spec...  15.1 us
    unnamed x49, local copies, waits for them, and re-layouts  12.6 us
    pallas_call x2, Pallas kernels, weight(): pl.pallas_call(weight_kernel, grid_spec=prefetched(1, (depth // width,),...  12.1 us
    pallas_call x2, Pallas kernels, backward(): pl.pallas_call(backward_kernel, grid_spec=prefetched(2, (heads,), [hs, ts...  11.2 us
  transfers between devices with their start and end apart: 18, of which 9 were waited for; matrix products, arithmetic and copies ran while one was open for 3% of the time, Pallas kernels for 22%

profile of v4, /device:TPU:1, one launch (start us, length us, event | category | flops | bytes accessed | tf_op | source)
XLA Modules:
  0.0 219.4 jit_solution(11716302912611322348)
XLA Ops:
  1.9 2.5 %collective-permute-start = (bf16[128,2560]{1,0:T(8,128)(2,1)S(1)}, bf16[128,2560]{1,0:T(8,128)(2,1)}, u32[]{:S(2)}, u32[]{:S(2)}) collective-permute-start(bf16[128,2560]{1,0:T(8,128)(2,1)S(1)} %slice.6), channel_id=1, source_target_pairs={{0,2},{2,4},{4,6},{6,0},{1,3},{3,5},{5,7},{7,1},{8,10},{10,12},{12... | collective-permute-start | bytes 1966088 | tf_op jit(solution)/shard_map/ppermute | solution.py:363
  4.4 16.3 %collective-permute-done.refs_2_ = bf16[128,2560]{1,0:T(8,128)(2,1)} collective-permute-done((bf16[128,2560]{1,0:T(8,128)(2,1)S(1)}, bf16[128,2560]{1,0:T(8,128)(2,1)}, u32[]{:S(2)}, u32[]{:S(2)}) %collective-permute-start) | collective-permute-done | bytes 655392 | tf_op jit(solution)/shard_map/ppermute | solution.py:363
  22.9 14.1 %collective-permute-done.1.refs_4_ = bf16[128,2560]{1,0:T(8,128)(2,1)} collective-permute-done((bf16[128,2560]{1,0:T(8,128)(2,1)}, bf16[128,2560]{1,0:T(8,128)(2,1)}, u32[]{:S(2)}, u32[]{:S(2)}) %collective-permute-start.1) | collective-permute-done | bytes 655392 | tf_op jit(solution)/shard_map/ppermute | solution.py:363
  39.0 3.0 %collective-permute-start.7 = (bf16[128,2560]{1,0:T(8,128)(2,1)}, bf16[128,2560]{1,0:T(8,128)(2,1)}, u32[]{:S(2)}, u32[]{:S(2)}) collective-permute-start(bf16[128,2560]{1,0:T(8,128)(2,1)} %collective-permute-done.refs_2_), channel_id=1, source_target_pairs={{0,1},{1,0},{2,3},{3,2},{4,5},{5,4},{6,7},{7,6},{8,9},{9,8},{10,11... | collective-permute-start | bytes 1966088 | tf_op jit(solution)/shard_map/ppermute | solution.py:29
  42.0 10.4 %collective-permute-done.9.refs_6_ = bf16[128,2560]{1,0:T(8,128)(2,1)} collective-permute-done((bf16[128,2560]{1,0:T(8,128)(2,1)}, bf16[128,2560]{1,0:T(8,128)(2,1)}, u32[]{:S(2)}, u32[]{:S(2)}) %collective-permute-start.9) | collective-permute-done | bytes 655392 | tf_op jit(solution)/shard_map/ppermute | solution.py:363
  52.4 7.3 %collective-permute-start.10 = (bf16[128,2560]{1,0:T(8,128)(2,1)}, bf16[128,2560]{1,0:T(8,128)(2,1)}, u32[]{:S(2)}, u32[]{:S(2)}) collective-permute-start(bf16[128,2560]{1,0:T(8,128)(2,1)} %collective-permute-done.9.refs_6_), channel_id=1, source_target_pairs={{0,1},{1,0},{2,3},{3,2},{4,5},{5,4},{6,7},{7,6},{8,9},{9,8},{10,11... | collective-permute-start | bytes 1966088 | tf_op jit(solution)/shard_map/ppermute | solution.py:29
  59.7 6.7 %collective-permute-done.2.refs_2_ = bf16[128,2560]{1,0:T(8,128)(2,1)} collective-permute-done((bf16[128,2560]{1,0:T(8,128)(2,1)}, bf16[128,2560]{1,0:T(8,128)(2,1)}, u32[]{:S(2)}, u32[]{:S(2)}) %collective-permute-start.2) | collective-permute-done | bytes 655392 | tf_op jit(solution)/shard_map/ppermute | solution.py:363
  68.9 6.1 %forward.1 = (bf16[3,8,512,128]{3,2,1,0:T(8,128)(2,1)S(1)}, bf16[1024,384]{1,0:T(8,128)(2,1)S(1)}, bf16[1024,384]{1,0:T(8,128)(2,1)S(1)}, bf16[384,1024]{1,0:T(8,128)(2,1)S(1)}) custom-call(s32[3]{0:T(128)S(1)} %pad_add_fusion.here_ref, s32[32,8]{1,0:T(8,128)S(1)} %copy.23.ids_ref, bf16[1024,384]{1,0:T(8,128)(2,1)S(1)} %copy-done.4, ...), custom_call_target="tpu_custom_call" | custom-call | flops 805306368 | bytes 7864320 | tf_op jit(solution)/shard_map/forward/pallas_call | solution.py:165
  78.5 6.3 %weight.3 = bf16[16,160,384]{2,1,0:T(8,128)(2,1)} custom-call(s32[3]{0:T(128)S(1)} %pad_add_fusion.here_ref, bf16[128,5120]{1,0:T(8,128)(2,1)S(1)} %copy-done, bf16[128,5120]{1,0:T(8,128)(2,1)S(1)} %collective-permute-done.6.refs_1_, bf16[128,2560]{1,0:T(8,128)(2,1)} %collective-permute-done.refs_2_, bf16[128,2560]{1,0:T(8,128)(2,1)} %collective-permute-done.7.refs_3_, ...), custom_call_target="tpu_custom_call" | custom-call | flops 2013265920 | bytes 7995392 | tf_op jit(solution)/shard_map/weight/pallas_call | solution.py:331
  85.6 9.5 %all-to-all-start.1 = ((bf16[16,160,384]{2,1,0:T(8,128)(2,1)}), bf16[16,160,384]{2,1,0:T(8,128)(2,1)}, u32[]{:S(2)}, u32[]{:S(2)}) async-start(bf16[16,160,384]{2,1,0:T(8,128)(2,1)} %weight.3), calls=%async_computation.1 | async-start | bytes 3932160 | tf_op jit(solution)/shard_map/all_to_all | solution.py:385
  95.2 3.3 %collective-permute-start.11 = (bf16[128,2560]{1,0:T(8,128)(2,1)}, bf16[128,2560]{1,0:T(8,128)(2,1)S(1)}, u32[]{:S(2)}, u32[]{:S(2)}) collective-permute-start(bf16[128,2560]{1,0:T(8,128)(2,1)} %collective-permute-done.2.refs_2_), channel_id=1, source_target_pairs={{0,1},{1,0},{2,3},{3,2},{4,5},{5,4},{6,7},{7,6},{8,9},{9,8},{10,11... | collective-permute-start | bytes 1966088 | tf_op jit(solution)/shard_map/ppermute | solution.py:29
  98.7 11.7 %collective-permute-done.4.refs_0_.refs_6_ = bf16[128,2560]{1,0:T(8,128)(2,1)S(1)} collective-permute-done((bf16[128,2560]{1,0:T(8,128)(2,1)}, bf16[128,2560]{1,0:T(8,128)(2,1)S(1)}, u32[]{:S(2)}, u32[]{:S(2)}) %collective-permute-start.4) | collective-permute-done | bytes 655392 | tf_op jit(solution)/shard_map/ppermute | solution.py:363
  110.4 4.0 %collective-permute-start.5 = (bf16[128,2560]{1,0:T(8,128)(2,1)S(1)}, bf16[128,2560]{1,0:T(8,128)(2,1)S(1)}, u32[]{:S(2)}, u32[]{:S(2)}) collective-permute-start(bf16[128,2560]{1,0:T(8,128)(2,1)S(1)} %collective-permute-done.4.refs_0_.refs_6_), channel_id=1, source_target_pairs={{0,1},{1,0},{2,3},{3,2},{4,5},{5,4},{6,7},{7,6},{8,9},{9,8},{10,11... | collective-permute-start | bytes 1966088 | tf_op jit(solution)/shard_map/ppermute | solution.py:29
  117.3 5.8 %weight.2 = bf16[16,160,384]{2,1,0:T(8,128)(2,1)} custom-call(s32[3]{0:T(128)S(1)} %pad_add_fusion.here_ref, bf16[128,5120]{1,0:T(8,128)(2,1)S(1)} %copy-done, bf16[128,5120]{1,0:T(8,128)(2,1)S(1)} %collective-permute-done.6.refs_1_, bf16[128,2560]{1,0:T(8,128)(2,1)} %collective-permute-done.2.refs_2_, ...), custom_call_target="tpu_custom_call" | custom-call | flops 2013265920 | bytes 7995392 | tf_op jit(solution)/shard_map/weight/pallas_call | solution.py:331
  126.4 6.7 %all-to-all-start = ((bf16[16,160,384]{2,1,0:T(8,128)(2,1)}), bf16[16,160,384]{2,1,0:T(8,128)(2,1)}, u32[]{:S(2)}, u32[]{:S(2)}) async-start(bf16[16,160,384]{2,1,0:T(8,128)(2,1)} %weight.2), calls=%async_computation | async-start | bytes 3932160 | tf_op jit(solution)/shard_map/all_to_all | solution.py:385
  133.1 7.0 %project.3.refs_7_.refs_3_ = f32[1024,384]{1,0:T(8,128)} custom-call(s32[3]{0:T(128)S(1)} %pad_add_fusion.here_ref, bf16[128,5120]{1,0:T(8,128)(2,1)S(1)} %copy-done, bf16[128,5120]{1,0:T(8,128)(2,1)S(1)} %collective-permute-done.6.refs_1_, bf16[128,2560]{1,0:T(8,128)(2,1)} %collective-permute-done.refs_2_, ...), custom_call_target="tpu_custom_call" | custom-call | flops 2013265920 | bytes 10354688 | tf_op jit(solution)/shard_map/project/pallas_call | solution.py:302
  141.5 4.8 %project.4.refs_4_ = bf16[1024,384]{1,0:T(8,128)(2,1)S(1)} custom-call(s32[3]{0:T(128)S(1)} %pad_add_fusion.here_ref, bf16[128,5120]{1,0:T(8,128)(2,1)S(1)} %copy-done, bf16[128,5120]{1,0:T(8,128)(2,1)S(1)} %collective-permute-done.6.refs_1_, bf16[128,2560]{1,0:T(8,128)(2,1)} %collective-permute-done.2.refs_2_, bf16[128,2560]{1,0:T(8,128)(2,1)S(1)} %copy-done.16, ...), custom_call_target="tpu_custom_call" | custom-call | flops 1509949440 | bytes 8257536 | tf_op jit(solution)/shard_map/project/pallas_call | solution.py:302
  146.4 3.3 %project.5.g_ref = bf16[1024,384]{1,0:T(8,128)(2,1)S(1)} custom-call(s32[3]{0:T(128)S(1)} %pad_add_fusion.here_ref, bf16[128,2560]{1,0:T(8,128)(2,1)S(1)} %copy-done.14, bf16[128,2560]{1,0:T(8,128)(2,1)S(1)} %copy-done.20, bf16[384,5120]{1,0:T(8,128)(2,1)} %refs_2_.1, f32[1024,384]{1,0:T(8,128)S(1)} %copy-done.1, ...), custom_call_target="tpu_custom_call", output_to_operand_aliasing={{}: (5, {})} | custom-call | flops 503316480 | bytes 4063232 | tf_op jit(solution)/shard_map/project/pallas_call | solution.py:302
  149.7 7.0 %backward.2 = (bf16[1024,384]{1,0:T(8,128)(2,1)}, bf16[1024,384]{1,0:T(8,128)(2,1)}, bf16[1024,384]{1,0:T(8,128)(2,1)}, bf16[3,512,256]{2,1,0:T(8,128)(2,1)S(1)}) custom-call(s32[3]{0:T(128)S(1)} %pad_add_fusion.here_ref, s32[32,8]{1,0:T(8,128)S(1)} %copy.23.ids_ref, bf16[1024,384]{1,0:T(8,128)(2,1)S(1)} %copy-done.4, bf16[384,1024]{1,0:T(8,128)(2,1)S(1)} %copy-done.10, ...), custom_call_target="tpu_custom_call" | custom-call | flops 1073741824 | bytes 7077888 | tf_op jit(solution)/shard_map/backward/pallas_call | solution.py:198
  156.8 5.0 %collective-permute-start.13 = (bf16[3,512,256]{2,1,0:T(8,128)(2,1)S(1)}, bf16[3,512,256]{2,1,0:T(8,128)(2,1)S(1)}, u32[]{:S(2)}, u32[]{:S(2)}) collective-permute-start(bf16[3,512,256]{2,1,0:T(8,128)(2,1)S(1)} %get-tuple-element.35), channel_id=1, source_target_pairs={{0,128},{128,0},{1,129},{129,1},{2,130},{130,2},{3,131},{131,3},{4... | collective-permute-start | bytes 2359304 | tf_op jit(solution)/shard_map/ppermute | solution.py:29
  161.7 4.2 %backward.3 = (bf16[1024,384]{1,0:T(8,128)(2,1)}, bf16[1024,384]{1,0:T(8,128)(2,1)}, bf16[1024,384]{1,0:T(8,128)(2,1)}, bf16[3,512,128]{2,1,0:T(8,128)(2,1)S(1)}) custom-call(s32[3]{0:T(128)S(1)} %pad_add_fusion.here_ref, s32[32,8]{1,0:T(8,128)S(1)} %copy.23.ids_ref, ...), custom_call_target="tpu_custom_call", output_to_operand_aliasing={{0}: (8, {}), {1}: (9, {}), {2}: (10, {})} | custom-call | flops 536870912 | bytes 3538944 | tf_op jit(solution)/shard_map/backward/pallas_call | solution.py:198
  170.1 5.1 %collective-permute-start.15 = (bf16[160,384]{1,0:T(8,128)(2,1)S(1)}, bf16[160,384]{1,0:T(8,128)(2,1)S(1)}, u32[]{:S(2)}, u32[]{:S(2)}) collective-permute-start(bf16[160,384]{1,0:T(8,128)(2,1)S(1)} %select_convert_fusion), channel_id=1, source_target_pairs={{0,128},{128,0},{1,129},{129,1},{2,130},{130,2},{3,131},{131,3},{4... | collective-permute-start | bytes 368648 | tf_op jit(solution)/shard_map/ppermute | solution.py:29
  175.1 22.2 %collective-permute-done.13.refs_3_ = bf16[3,512,256]{2,1,0:T(8,128)(2,1)S(1)} collective-permute-done((bf16[3,512,256]{2,1,0:T(8,128)(2,1)S(1)}, bf16[3,512,256]{2,1,0:T(8,128)(2,1)S(1)}, u32[]{:S(2)}, u32[]{:S(2)}) %collective-permute-start.13) | collective-permute-done | bytes 786464 | tf_op jit(solution)/shard_map/ppermute | solution.py:29
  198.8 17.2 %collective-permute-done.14.refs_3_ = bf16[3,512,128]{2,1,0:T(8,128)(2,1)S(1)} collective-permute-done((bf16[3,512,128]{2,1,0:T(8,128)(2,1)S(1)}, bf16[3,512,128]{2,1,0:T(8,128)(2,1)S(1)}, u32[]{:S(2)}, u32[]{:S(2)}) %collective-permute-start.14) | collective-permute-done | bytes 393248 | tf_op jit(solution)/shard_map/ppermute | solution.py:29
  (78 shorter events, 28.9 us)
Async XLA Ops:
  0.6 65.9 %copy-start.23 = (s32[32,8]{0,1:T(8,128)S(1)}, s32[32,8]{0,1:T(8,128)}, u32[]{:S(2)}) copy-start(s32[32,8]{0,1:T(8,128)} %param.12) | copy-start | bytes 3076
  0.6 66.0 %copy-start.4 = (bf16[1024,384]{1,0:T(8,128)(2,1)S(1)}, bf16[1024,384]{1,0:T(8,128)(2,1)}, u32[]{:S(2)}) copy-start(bf16[1024,384]{1,0:T(8,128)(2,1)} %q_ref.5) | copy-start | bytes 2359300
  1.9 76.6 %copy-start = (bf16[128,5120]{1,0:T(8,128)(2,1)S(1)}, bf16[128,5120]{1,0:T(8,128)(2,1)}, u32[]{:S(2)}) copy-start(bf16[128,5120]{1,0:T(8,128)(2,1)} %refs_0_.7) | copy-start | bytes 3932164
  1.9 18.9 %collective-permute-start = (bf16[128,2560]{1,0:T(8,128)(2,1)S(1)}, bf16[128,2560]{1,0:T(8,128)(2,1)}, u32[]{:S(2)}, u32[]{:S(2)}) collective-permute-start(bf16[128,2560]{1,0:T(8,128)(2,1)S(1)} %slice.6), channel_id=1, source_target_pairs={{0,2},{2,4},{4,6},{6,0},{1,3},{3,5},{5,7},{7,1},{8,10},{10,12},{12... | collective-permute-start | bytes 1966088 | tf_op jit(solution)/shard_map/ppermute | solution.py:363
  20.7 16.2 %collective-permute-start.1 = (bf16[128,2560]{1,0:T(8,128)(2,1)}, bf16[128,2560]{1,0:T(8,128)(2,1)}, u32[]{:S(2)}, u32[]{:S(2)}) collective-permute-start(bf16[128,2560]{1,0:T(8,128)(2,1)} %collective-permute-done.refs_2_), channel_id=1, source_target_pairs={{0,2},{2,4},{4,6},{6,0},{1,3},{3,5},{5,7},{7,1},{8,10},{10,12},{12... | collective-permute-start | bytes 1966088 | tf_op jit(solution)/shard_map/ppermute | solution.py:363
  20.8 57.7 %collective-permute-start.6 = (bf16[128,5120]{1,0:T(8,128)(2,1)}, bf16[128,5120]{1,0:T(8,128)(2,1)S(1)}, u32[]{:S(2)}, u32[]{:S(2)}) collective-permute-start(bf16[128,5120]{1,0:T(8,128)(2,1)} %refs_0_.7), channel_id=1, source_target_pairs={{0,1},{1,0},{2,3},{3,2},{4,5},{5,4},{6,7},{7,6},{8,9},{9,8},{10,11... | collective-permute-start | bytes 3932168 | tf_op jit(solution)/shard_map/ppermute | solution.py:29
  37.0 15.4 %collective-permute-start.9 = (bf16[128,2560]{1,0:T(8,128)(2,1)}, bf16[128,2560]{1,0:T(8,128)(2,1)}, u32[]{:S(2)}, u32[]{:S(2)}) collective-permute-start(bf16[128,2560]{1,0:T(8,128)(2,1)} %collective-permute-done.1.refs_4_), channel_id=1, source_target_pairs={{0,2},{2,4},{4,6},{6,0},{1,3},{3,5},{5,7},{7,1},{8,10},{10,12},{12... | collective-permute-start | bytes 1966088 | tf_op jit(solution)/shard_map/ppermute | solution.py:363
  39.0 27.5 %collective-permute-start.2 = (bf16[128,2560]{1,0:T(8,128)(2,1)}, bf16[128,2560]{1,0:T(8,128)(2,1)}, u32[]{:S(2)}, u32[]{:S(2)}) collective-permute-start(bf16[128,2560]{1,0:T(8,128)(2,1)} %slice.7), channel_id=1, source_target_pairs={{0,2},{2,4},{4,6},{6,0},{1,3},{3,5},{5,7},{7,1},{8,10},{10,12},{12... | collective-permute-start | bytes 1966088 | tf_op jit(solution)/shard_map/ppermute | solution.py:363
  39.0 39.4 %collective-permute-start.7 = (bf16[128,2560]{1,0:T(8,128)(2,1)}, bf16[128,2560]{1,0:T(8,128)(2,1)}, u32[]{:S(2)}, u32[]{:S(2)}) collective-permute-start(bf16[128,2560]{1,0:T(8,128)(2,1)} %collective-permute-done.refs_2_), channel_id=1, source_target_pairs={{0,1},{1,0},{2,3},{3,2},{4,5},{5,4},{6,7},{7,6},{8,9},{9,8},{10,11... | collective-permute-start | bytes 1966088 | tf_op jit(solution)/shard_map/ppermute | solution.py:29
  42.0 36.4 %collective-permute-start.8 = (bf16[128,2560]{1,0:T(8,128)(2,1)}, bf16[128,2560]{1,0:T(8,128)(2,1)}, u32[]{:S(2)}, u32[]{:S(2)}) collective-permute-start(bf16[128,2560]{1,0:T(8,128)(2,1)} %collective-permute-done.1.refs_4_), channel_id=1, source_target_pairs={{0,1},{1,0},{2,3},{3,2},{4,5},{5,4},{6,7},{7,6},{8,9},{9,8},{10,11... | collective-permute-start | bytes 1966088 | tf_op jit(solution)/shard_map/ppermute | solution.py:29
  52.4 26.0 %collective-permute-start.10 = (bf16[128,2560]{1,0:T(8,128)(2,1)}, bf16[128,2560]{1,0:T(8,128)(2,1)}, u32[]{:S(2)}, u32[]{:S(2)}) collective-permute-start(bf16[128,2560]{1,0:T(8,128)(2,1)} %collective-permute-done.9.refs_6_), channel_id=1, source_target_pairs={{0,1},{1,0},{2,3},{3,2},{4,5},{5,4},{6,7},{7,6},{8,9},{9,8},{10,11... | collective-permute-start | bytes 1966088 | tf_op jit(solution)/shard_map/ppermute | solution.py:29
  66.4 28.7 %collective-permute-start.3 = (bf16[128,2560]{1,0:T(8,128)(2,1)}, bf16[128,2560]{1,0:T(8,128)(2,1)}, u32[]{:S(2)}, u32[]{:S(2)}) collective-permute-start(bf16[128,2560]{1,0:T(8,128)(2,1)} %collective-permute-done.2.refs_2_), channel_id=1, source_target_pairs={{0,2},{2,4},{4,6},{6,0},{1,3},{3,5},{5,7},{7,1},{8,10},{10,12},{12... | collective-permute-start | bytes 1966088 | tf_op jit(solution)/shard_map/ppermute | solution.py:363
  85.6 40.8 %all-to-all-start.1 = ((bf16[16,160,384]{2,1,0:T(8,128)(2,1)}), bf16[16,160,384]{2,1,0:T(8,128)(2,1)}, u32[]{:S(2)}, u32[]{:S(2)}) async-start(bf16[16,160,384]{2,1,0:T(8,128)(2,1)} %weight.3), calls=%async_computation.1 | async-start | bytes 3932160 | tf_op jit(solution)/shard_map/all_to_all | solution.py:385
  95.2 15.2 %collective-permute-start.4 = (bf16[128,2560]{1,0:T(8,128)(2,1)}, bf16[128,2560]{1,0:T(8,128)(2,1)S(1)}, u32[]{:S(2)}, u32[]{:S(2)}) collective-permute-start(bf16[128,2560]{1,0:T(8,128)(2,1)} %collective-permute-done.3.refs_4_), channel_id=1, source_target_pairs={{0,2},{2,4},{4,6},{6,0},{1,3},{3,5},{5,7},{7,1},{8,10},{10,12},{12... | collective-permute-start | bytes 1966088 | tf_op jit(solution)/shard_map/ppermute | solution.py:363
  95.2 19.1 %collective-permute-start.11 = (bf16[128,2560]{1,0:T(8,128)(2,1)}, bf16[128,2560]{1,0:T(8,128)(2,1)S(1)}, u32[]{:S(2)}, u32[]{:S(2)}) collective-permute-start(bf16[128,2560]{1,0:T(8,128)(2,1)} %collective-permute-done.2.refs_2_), channel_id=1, source_target_pairs={{0,1},{1,0},{2,3},{3,2},{4,5},{5,4},{6,7},{7,6},{8,9},{9,8},{10,11... | collective-permute-start | bytes 1966088 | tf_op jit(solution)/shard_map/ppermute | solution.py:29
  98.6 15.8 %collective-permute-start.12 = (bf16[128,2560]{1,0:T(8,128)(2,1)}, bf16[128,2560]{1,0:T(8,128)(2,1)S(1)}, u32[]{:S(2)}, u32[]{:S(2)}) collective-permute-start(bf16[128,2560]{1,0:T(8,128)(2,1)} %collective-permute-done.3.refs_4_), channel_id=1, source_target_pairs={{0,1},{1,0},{2,3},{3,2},{4,5},{5,4},{6,7},{7,6},{8,9},{9,8},{10,11... | collective-permute-start | bytes 1966088 | tf_op jit(solution)/shard_map/ppermute | solution.py:29
  110.4 5.7 %collective-permute-start.5 = (bf16[128,2560]{1,0:T(8,128)(2,1)S(1)}, bf16[128,2560]{1,0:T(8,128)(2,1)S(1)}, u32[]{:S(2)}, u32[]{:S(2)}) collective-permute-start(bf16[128,2560]{1,0:T(8,128)(2,1)S(1)} %collective-permute-done.4.refs_0_.refs_6_), channel_id=1, source_target_pairs={{0,1},{1,0},{2,3},{3,2},{4,5},{5,4},{6,7},{7,6},{8,9},{9,8},{10,11... | collective-permute-start | bytes 1966088 | tf_op jit(solution)/shard_map/ppermute | solution.py:29
  126.4 41.7 %all-to-all-start = ((bf16[16,160,384]{2,1,0:T(8,128)(2,1)}), bf16[16,160,384]{2,1,0:T(8,128)(2,1)}, u32[]{:S(2)}, u32[]{:S(2)}) async-start(bf16[16,160,384]{2,1,0:T(8,128)(2,1)} %weight.2), calls=%async_computation | async-start | bytes 3932160 | tf_op jit(solution)/shard_map/all_to_all | solution.py:385
  133.1 7.0 %copy-start.16 = (bf16[128,2560]{1,0:T(8,128)(2,1)S(1)}, bf16[128,2560]{1,0:T(8,128)(2,1)}, u32[]{:S(2)}) copy-start(bf16[128,2560]{1,0:T(8,128)(2,1)} %copy-done.15) | copy-start | bytes 1966084
  133.1 7.0 %copy-start.18 = (bf16[128,2560]{1,0:T(8,128)(2,1)S(1)}, bf16[128,2560]{1,0:T(8,128)(2,1)}, u32[]{:S(2)}) copy-start(bf16[128,2560]{1,0:T(8,128)(2,1)} %copy-done.17) | copy-start | bytes 1966084
  156.8 40.6 %collective-permute-start.13 = (bf16[3,512,256]{2,1,0:T(8,128)(2,1)S(1)}, bf16[3,512,256]{2,1,0:T(8,128)(2,1)S(1)}, u32[]{:S(2)}, u32[]{:S(2)}) collective-permute-start(bf16[3,512,256]{2,1,0:T(8,128)(2,1)S(1)} %get-tuple-element.35), channel_id=1, source_target_pairs={{0,128},{128,0},{1,129},{129,1},{2,130},{130,2},{3,131},{131,3},{4... | collective-permute-start | bytes 2359304 | tf_op jit(solution)/shard_map/ppermute | solution.py:29
  165.9 50.1 %collective-permute-start.14 = (bf16[3,512,128]{2,1,0:T(8,128)(2,1)S(1)}, bf16[3,512,128]{2,1,0:T(8,128)(2,1)S(1)}, u32[]{:S(2)}, u32[]{:S(2)}) collective-permute-start(bf16[3,512,128]{2,1,0:T(8,128)(2,1)S(1)} %get-tuple-element.39), channel_id=1, source_target_pairs={{0,128},{128,0},{1,129},{129,1},{2,130},{130,2},{3,131},{131,3},{4... | collective-permute-start | bytes 1179656 | tf_op jit(solution)/shard_map/ppermute | solution.py:29
  168.2 29.2 %copy-start.21 = (s32[32]{0:T(128)S(1)}, s32[32]{0:T(128)}, u32[]{:S(2)}) copy-start(s32[32]{0:T(128)} %counts_ref.3) | copy-start | bytes 388
  170.1 48.6 %collective-permute-start.15 = (bf16[160,384]{1,0:T(8,128)(2,1)S(1)}, bf16[160,384]{1,0:T(8,128)(2,1)S(1)}, u32[]{:S(2)}, u32[]{:S(2)}) collective-permute-start(bf16[160,384]{1,0:T(8,128)(2,1)S(1)} %select_convert_fusion), channel_id=1, source_target_pairs={{0,128},{128,0},{1,129},{129,1},{2,130},{130,2},{3,131},{131,3},{4... | collective-permute-start | bytes 368648 | tf_op jit(solution)/shard_map/ppermute | solution.py:29
  (18 other events, 35.5 us)
